TPU v7x, 1024 devices: a whole 4x8x16 slice. The times are simulated.
1024 devices in a mesh: ens: 16 (over y_lo, x, core), polar: 64 (over z, y_hi).
Axes of the slice: x: 4, y: 8 (y_hi: 4, y_lo: 2; y = y_hi * 2 + y_lo), z: 16, core: 2. Of those that a mesh axis runs over, the one named last changes fastest.
Arguments:
- field: bfloat16 [16, 384, 96, 720], P('ens', 'polar'), may hold values from -6 to 6
- target: bfloat16 [384, 384, 720], P('polar'), may hold values from -6 to 6
- slot_orders: int32 [384], replicated, may hold values from 0 to 383, each once
- analysis: bfloat16 [384, 384, 360], P('polar'), may hold values from -0.3125 to 0.3125
- synthesis: bfloat16 [384, 360, 384], P('polar'), may hold values from -0.3125 to 0.3125
- degree_filter: float32 [384, 360], replicated, may hold values from -4 to 4
Outputs:
- prediction: bfloat16 [16, 384, 96, 720], P('ens', 'polar')
- gradient: bfloat16 [16, 384, 96, 720], P('ens', 'polar')
Inputs may be any that keep to these rules, and one draw needn't show every extreme that they name: `slot_orders`: each slot number 0 to 383 appears once; a slot whose order is 360 or more is empty.
All inputs are finite; a program needn't handle non-finite values.
Results may differ from a plain program's by a relative error of at most 0.006.
Values may be sent and summed in bfloat16 or wider, within the bound.
No kernel may reach another device: no remote copies, remote signals or barrier semaphores. Data moves between devices by JAX's collectives and lax.ppermute only.
A program may use at most 64 MiB of HBM per device.

v0:
```python
import math

import jax
import jax.numpy as jnp
from jax import lax
from jax.sharding import PartitionSpec as P

ENS = 4


smooth_sq = 0.25


def lon_tables(slot_orders, lon_count, degree_total):
    points = jnp.arange(lon_count, dtype=jnp.int32)
    phase = slot_orders[:, None] * points[None, :] % lon_count
    angle = phase.astype(jnp.float32) * (2.0 * math.pi / lon_count)
    live = (slot_orders < degree_total).astype(jnp.float32)[:, None]
    cosine = jnp.cos(angle) * live
    sine = jnp.sin(angle) * live
    paired = jnp.stack([cosine, -sine], 1)
    forward = (paired / math.sqrt(lon_count)).astype(jnp.bfloat16)
    inverse = (paired / math.sqrt(degree_total)).astype(jnp.bfloat16)
    return (forward, inverse)


def kernel_slope(diff):
    return diff / jnp.sqrt(diff * diff + smooth_sq)


def crps_slope(grouped, observed, group_count):
    rest = grouped.shape[1:]
    values = grouped.reshape((group_count, ENS) + rest).astype(jnp.float32)
    own_term = kernel_slope(values - observed.astype(jnp.float32)[:, None])

    def add_member(summed, other):
        return (summed + kernel_slope(values - other[:, None]), None)

    pair_sum, unused = lax.scan(add_member, jnp.zeros_like(values), jnp.moveaxis(values, 1, 0))
    slopes = (own_term - pair_sum / ENS).astype(jnp.bfloat16)
    return slopes.reshape(grouped.shape)


def body(field, target, slot_orders, analysis, synthesis, degree_filter):
    lat_count, chan_count, lon_count = (field.shape[1], field.shape[2], field.shape[3])
    slot_count = slot_orders.shape[0]
    ord_local, degree_total = (analysis.shape[0], analysis.shape[2])
    forward, inverse = lon_tables(slot_orders, lon_count, degree_total)
    flat = field.reshape(lat_count * chan_count, lon_count)
    spectral = jnp.dot(
        flat, forward.reshape(slot_count * 2, lon_count).T, preferred_element_type=jnp.float32
    ).astype(jnp.bfloat16)
    spectral = spectral.reshape(lat_count, chan_count, slot_count, 2).transpose(2, 3, 0, 1)
    offset = lax.axis_index("polar") * ord_local
    mine = lax.dynamic_slice_in_dim(slot_orders, offset, ord_local)
    degrees = jnp.arange(degree_total, dtype=jnp.int32)
    keeping = (degrees[None, :] >= mine[:, None]).astype(jnp.float32)
    slab_index = lax.axis_index("ens")
    slab_number = lax.axis_size("ens")
    group_count = slab_number // ENS
    filter_rows = lax.dynamic_slice_in_dim(
        degree_filter, slab_index // ENS * chan_count, chan_count, 0
    )
    scaling = keeping[:, None, :, None] * filter_rows.T[None, None]
    coeffs = jnp.einsum(
        "sptc,stl->splc",
        lax.all_to_all(spectral, "polar", split_axis=0, concat_axis=2, tiled=True),
        analysis,
        preferred_element_type=jnp.float32,
    )
    scaled = (coeffs * scaling).astype(jnp.bfloat16)
    bands = jnp.einsum(
        "splc,slt->sptc", scaled, synthesis, preferred_element_type=jnp.float32
    ).astype(jnp.bfloat16)
    result_value = lax.all_to_all(bands, "polar", split_axis=2, concat_axis=0, tiled=True)
    synth = jnp.einsum("sptc,spk->tck", result_value, inverse, preferred_element_type=jnp.float32)
    prediction = (field[0].astype(jnp.float32) + synth).astype(jnp.bfloat16)[None]
    width = lon_count // slab_number
    blocks = prediction[0].reshape(lat_count, chan_count, slab_number, width)
    blocks = blocks.transpose(2, 0, 1, 3).reshape(slab_number, lat_count, chan_count * width)
    grouped = lax.all_to_all(blocks, "ens", split_axis=0, concat_axis=0, tiled=True)
    regrouped = target.reshape(lat_count, group_count, chan_count, lon_count)
    observed = lax.dynamic_slice_in_dim(regrouped, slab_index * width, width, 3)
    observed = observed.transpose(1, 0, 2, 3).reshape(group_count, lat_count, chan_count * width)
    slopes = crps_slope(grouped, observed, group_count)
    returned = lax.all_to_all(slopes, "ens", split_axis=0, concat_axis=0, tiled=True)
    returned = returned.reshape(slab_number, lat_count, chan_count, width).transpose(1, 2, 0, 3)
    gradient = returned.reshape(lat_count, chan_count, lon_count)[None]
    return (prediction, gradient)


def solution(mesh):
    in_specs = (
        P("ens", "polar", None, None),
        P("polar", None, None),
        P(),
        P("polar", None, None),
        P("polar", None, None),
        P(),
    )
    out_specs = (P("ens", "polar", None, None), P("ens", "polar", None, None))
    return jax.shard_map(body, mesh=mesh, in_specs=in_specs, out_specs=out_specs, check_vma=False)
```

profile of v0, /device:TPU:1, one launch (start us, length us, event | category | flops | bytes accessed | tf_op | source)
XLA Modules:
  0.0 286.8 jit_solution(18395085907876502200)
XLA Ops:
  1.5 5.4 %cosine_multiply_fusion = (f32[384,1,720]{0,2,1:T(8,128)S(1)}, f32[384,1,720]{0,2,1:T(8,128)S(1)}) fusion(f32[384]{0:T(512)S(1)} %compare_convert_fusion, s32[384]{0:T(512)} %param.10), kind=kLoop, calls=%fused_computation.28 | loop fusion | flops 3317760 | bytes 2214912 | tf_op jit(solution)/shard_map/mul | solution.py:19
  9.4 3.6 %copy.30 = bf16[384,2,720]{2,1,0:T(2,128)(2,1)S(1)} copy(bf16[384,2,720]{0,2,1:T(8,128)(2,1)} %multiply_convert_fusion.1) | data formatting | bytes 2211840 | tf_op jit(solution)/shard_map/convert_element_type | solution.py:22
  13.0 1.8 convert_element_type.91
  14.8 2.4 fusion.14
  18.6 2.8 reshape.195
  21.4 2.2 copy.32
  23.6 25.8 %all-to-all-start = ((bf16[384,2,6,96]{3,1,2,0:T(2,128)(2,1)}), bf16[384,2,6,96]{3,1,2,0:T(2,128)(2,1)S(1)}, u32[]{:S(2)}, u32[]{:S(2)}) async-start(bf16[384,2,6,96]{3,1,2,0:T(2,128)(2,1)} %copy.32), calls=%async_computation | async-start | bytes 2359296 | tf_op jit(solution)/shard_map/all_to_all | solution.py:67
  52.5 54.3 %all-to-all-done = bf16[384,2,6,96]{3,1,2,0:T(2,128)(2,1)S(1)} async-done(((bf16[384,2,6,96]{3,1,2,0:T(2,128)(2,1)}), bf16[384,2,6,96]{3,1,2,0:T(2,128)(2,1)S(1)}, u32[]{:S(2)}, u32[]{:S(2)}) %all-to-all-start) | async-done | bytes 884768 | tf_op jit(solution)/shard_map/all_to_all | solution.py:67
  106.8 1.8 copy.33
  108.6 4.3 %fusion.11 = bf16[6,2,384,96]{2,3,1,0:T(8,128)(2,1)} fusion(bf16[6,360,384]{2,1,0:T(8,128)(2,1)S(1)} %copy-done, bf16[6,384,360]{1,2,0:T(8,128)(2,1)} %param.11, bf16[6,2,384,96]{3,1,2,0:T(2,128)(2,1)} %bitcast.91, f32[6,360,96]{1,2,0:T(8,128)} %broadcast_multiply_fusion), kind=kOutput, calls=%fused_computation.17 | convolution fusion | flops 638281728 | bytes 5916672 | tf_op jit(solution)/shard_map/splc,slt->sptc/dot_general | solution.py:72
  113.0 3.5 %copy.36 = bf16[6,2,384,96]{3,1,0,2:T(2,128)(2,1)S(1)} copy(bf16[6,2,384,96]{2,3,1,0:T(8,128)(2,1)} %fusion.11) | data formatting | bytes 1769472 | tf_op jit(solution)/shard_map/convert_element_type | solution.py:74
  116.5 68.1 %all_to_all.46 = bf16[6,2,384,96]{3,1,0,2:T(2,128)(2,1)S(1)} all-to-all(bf16[6,2,384,96]{3,1,0,2:T(2,128)(2,1)S(1)} %copy.36), channel_id=1, replica_groups=mesh['ens'=16,'polar'=64] {'polar'}, dimensions={2} | all-to-all | bytes 1769472 | tf_op jit(solution)/shard_map/all_to_all | solution.py:75
  189.7 1.4 reshape_squeeze_broadcast_in_dim.3
  191.1 2.6 copy.53
  193.7 5.3 %reshape.207 = bf16[16,6,4320]{2,1,0:T(8,128)(2,1)} reshape(bf16[16,6,96,45]{3,2,1,0:T(8,128)(2,1)} %copy.53) | data formatting | bytes 1658880 | tf_op jit(solution)/shard_map/reshape | solution.py:80
  199.0 9.1 %all-to-all-start.2 = ((bf16[16,6,4320]{2,1,0:T(8,128)(2,1)}), bf16[16,6,4320]{2,1,0:T(8,128)(2,1)S(1)}, u32[]{:S(2)}, u32[]{:S(2)}) async-start(bf16[16,6,4320]{2,1,0:T(8,128)(2,1)} %reshape.207), calls=%async_computation.2 | async-start | bytes 2228224 | tf_op jit(solution)/shard_map/all_to_all | solution.py:81
  208.1 5.9 %copy.43 = bf16[6,384,720]{2,1,0:T(8,128)(2,1)} copy(bf16[6,384,720]{1,2,0:T(8,128)(2,1)} %param.9) | data formatting | bytes 6635520 | tf_op args[1]
  214.0 2.5 convert_bitcast_fusion
  216.5 2.8 reshape.202
  220.4 4.0 %all-to-all-done.2 = bf16[16,6,4320]{2,1,0:T(8,128)(2,1)S(1)} async-done(((bf16[16,6,4320]{2,1,0:T(8,128)(2,1)}), bf16[16,6,4320]{2,1,0:T(8,128)(2,1)S(1)}, u32[]{:S(2)}, u32[]{:S(2)}) %all-to-all-start.2) | async-done | bytes 829472 | tf_op jit(solution)/shard_map/all_to_all | solution.py:81
  224.4 1.5 convert_bitcast_fusion.1
  225.9 1.6 convert.4
  227.5 20.6 %while.11 = (s32[]{:T(128)}, f32[4,4,6,4320]{3,2,1,0:T(8,128)}, f32[4,4,6,4320]{3,2,0,1:T(8,128)}, f32[4,4,6,4320]{3,2,1,0:T(8,128)}, s32[]{:T(128)}, /*index=5*/s32[]{:T(128)}) while((s32[]{:T(128)}, f32[4,4,6,4320]{3,2,1,0:T(8,128)}, f32[4,4,6,4320]{3,2,0,1:T(8,128)}, f32[4,4,6,4320]{3,2,1,0:T(8,128)}, s32[]{:T(128)}, ...), condition=%wide.region_1.2_spmd.clone, body=%wide.region_0.1_spmd.clone.sunk | while | flops 2488323 | bytes 6220891 | solution.py:39
  228.6 3.6 %select_add_fusion.2 = f32[4,4,6,4320]{3,2,1,0:T(8,128)} fusion(f32[4,4,6,4320]{3,2,1,0:T(8,128)} %get-tuple-element.98, f32[4,4,6,4320]{3,2,1,0:T(8,128)} %get-tuple-element.106, f32[4,6,4320]{2,1,0:T(8,128)S(1)} %dynamic-slice_bitcast_fusion.3, pred[]{:T(512)S(6)} %compare.5), kind=kLoop, calls=%fused_computation.clone.1 | loop fusion | flops 2488320 | bytes 5391361 | tf_op jit(solution)/shard_map/while/body/eval_jaxpr/add | solution.py:37
  233.2 4.2 %select_add_fusion.2 = f32[4,4,6,4320]{3,2,1,0:T(8,128)} fusion(f32[4,4,6,4320]{3,2,1,0:T(8,128)} %get-tuple-element.98, f32[4,4,6,4320]{3,2,1,0:T(8,128)} %get-tuple-element.106, f32[4,6,4320]{2,1,0:T(8,128)S(1)} %dynamic-slice_bitcast_fusion.3, pred[]{:T(512)S(6)} %compare.5), kind=kLoop, calls=%fused_computation.clone.1 | loop fusion | flops 2488320 | bytes 5391361 | tf_op jit(solution)/shard_map/while/body/eval_jaxpr/add | solution.py:37
  238.6 4.2 %select_add_fusion.2 = f32[4,4,6,4320]{3,2,1,0:T(8,128)} fusion(f32[4,4,6,4320]{3,2,1,0:T(8,128)} %get-tuple-element.98, f32[4,4,6,4320]{3,2,1,0:T(8,128)} %get-tuple-element.106, f32[4,6,4320]{2,1,0:T(8,128)S(1)} %dynamic-slice_bitcast_fusion.3, pred[]{:T(512)S(6)} %compare.5), kind=kLoop, calls=%fused_computation.clone.1 | loop fusion | flops 2488320 | bytes 5391361 | tf_op jit(solution)/shard_map/while/body/eval_jaxpr/add | solution.py:37
  243.9 4.2 %select_add_fusion.2 = f32[4,4,6,4320]{3,2,1,0:T(8,128)} fusion(f32[4,4,6,4320]{3,2,1,0:T(8,128)} %get-tuple-element.98, f32[4,4,6,4320]{3,2,1,0:T(8,128)} %get-tuple-element.106, f32[4,6,4320]{2,1,0:T(8,128)S(1)} %dynamic-slice_bitcast_fusion.3, pred[]{:T(512)S(6)} %compare.5), kind=kLoop, calls=%fused_computation.clone.1 | loop fusion | flops 2488320 | bytes 5391361 | tf_op jit(solution)/shard_map/while/body/eval_jaxpr/add | solution.py:37
  248.1 2.3 subtract_convert_fusion
  250.4 20.3 %all_to_all.47 = bf16[16,6,4320]{2,1,0:T(8,128)(2,1)S(1)} all-to-all(bf16[16,6,4320]{2,1,0:T(8,128)(2,1)S(1)} %bitcast.92), channel_id=1, replica_groups=mesh['ens'=16,'polar'=64] {'ens'}, dimensions={0} | all-to-all | bytes 1658880 | tf_op jit(solution)/shard_map/all_to_all | solution.py:86
  270.8 7.3 %reshape.199 = bf16[16,6,96,45]{3,2,0,1:T(8,128)(2,1)} reshape(bf16[16,6,4320]{2,0,1:T(8,128)(2,1)S(1)} %copy.46) | data formatting | bytes 1658880 | tf_op jit(solution)/shard_map/reshape | solution.py:87
  278.1 4.0 %copy.54 = bf16[6,96,16,45]{3,2,1,0:T(8,128)(2,1)} copy(bf16[6,96,16,45]{3,1,2,0:T(8,128)(2,1)} %bitcast.85) | data formatting | bytes 1658880
  282.1 4.7 %reshape.208 = bf16[1,6,96,720]{3,2,1,0:T(8,128)(2,1)} reshape(bf16[6,96,16,45]{3,2,1,0:T(8,128)(2,1)} %copy.54) | data formatting | bytes 1658880
  (32 shorter events, 18.5 us)
Async XLA Ops:
  0.6 108.0 %copy-start = (bf16[6,360,384]{2,1,0:T(8,128)(2,1)S(1)}, bf16[6,360,384]{2,1,0:T(8,128)(2,1)}, u32[]{:S(2)}) copy-start(bf16[6,360,384]{2,1,0:T(8,128)(2,1)} %param.12) | copy-start | bytes 4976644
  6.8 1.0 copy-start.1
  6.8 1.4 copy-start.3
  23.6 83.2 %all-to-all-start = ((bf16[384,2,6,96]{3,1,2,0:T(2,128)(2,1)}), bf16[384,2,6,96]{3,1,2,0:T(2,128)(2,1)S(1)}, u32[]{:S(2)}, u32[]{:S(2)}) async-start(bf16[384,2,6,96]{3,1,2,0:T(2,128)(2,1)} %copy.32), calls=%async_computation | async-start | bytes 2359296 | tf_op jit(solution)/shard_map/all_to_all | solution.py:67
  116.5 68.9 %copy-start.6 = (bf16[1,6,96,720]{3,2,1,0:T(8,128)(2,1)S(1)}, bf16[1,6,96,720]{3,2,1,0:T(8,128)(2,1)}, u32[]{:S(2)}) copy-start(bf16[1,6,96,720]{3,2,1,0:T(8,128)(2,1)} %param.8) | copy-start | bytes 2488324
  184.6 1.2 copy-start.2
  184.6 1.6 copy-start.4
  187.4 0.9 copy-start.5
  199.0 25.5 %all-to-all-start.2 = ((bf16[16,6,4320]{2,1,0:T(8,128)(2,1)}), bf16[16,6,4320]{2,1,0:T(8,128)(2,1)S(1)}, u32[]{:S(2)}, u32[]{:S(2)}) async-start(bf16[16,6,4320]{2,1,0:T(8,128)(2,1)} %reshape.207), calls=%async_computation.2 | async-start | bytes 2228224 | tf_op jit(solution)/shard_map/all_to_all | solution.py:81
where the time goes:
time: 288 us; the launch traced here: 287 us
  blocking collectives  88.4 us (31%)
  local copies, waits for them, and re-layouts  63.9 us (22%)
  waiting for transfers between devices  58.4 us (20%)
  starting transfers between devices  34.9 us (12%)
  other arithmetic  32.5 us (11%)
  matrix products  7.94 us (3%)
    all_to_all x1, blocking collectives, body(): lax.all_to_all(bands, 'polar', split_axis=2, concat_axis=0, tiled=True)  68.1 us
    all_to_all x1, waiting for transfers between devices, body(): lax.all_to_all(spectral, 'polar', split_axis=0, concat_axis=2, tiled=True)  54.3 us
    all_to_all x1, starting transfers between devices, body(): lax.all_to_all(spectral, 'polar', split_axis=0, concat_axis=2, tiled=True)  25.8 us
    all_to_all x1, blocking collectives, body(): lax.all_to_all(slopes, 'ens', split_axis=0, concat_axis=0, tiled=True)  20.3 us
    unnamed x17, local copies, waits for them, and re-layouts  17.7 us
    add x4, other arithmetic, add_member(): return (summed + kernel_slope(values - other[:, None]), None)  16.2 us
    all_to_all x1, starting transfers between devices, body(): lax.all_to_all(blocks, 'ens', split_axis=0, concat_axis=0, tiled=True)  9.11 us
    reshape x2, local copies, waits for them, and re-layouts, body(): blocks.transpose(2, 0, 1, 3)  7.88 us
  transfers between devices with their start and end apart: 2, of which 2 were waited for; matrix products, arithmetic and copies ran while one was open for 5% of the time, Pallas kernels for 0%

commit v1 on v0

v1 whole, which is shorter than its diff:
```python
import functools
import math

import jax
import jax.numpy as jnp
from jax import lax
from jax.experimental import pallas as pl
from jax.experimental.pallas import tpu as pltpu
from jax.sharding import PartitionSpec as P

ENS = 4
BF = jnp.bfloat16
F32 = jnp.float32
smooth_sq = 0.25
LANES = 128


def turn_sine(turns):
    w = turns * (2.0 * math.pi)
    w2 = w * w
    poly = -2.5052108e-8 + w2 * 1.6059044e-10
    for coef in (2.7557319e-6, -1.9841270e-4, 8.3333333e-3, -1.6666667e-1, 1.0):
        poly = poly * w2 + coef
    return poly * w


def cosine_sine(orders, points, lon_count):
    product = orders * points
    phase = product - jnp.floor(product * (1.0 / lon_count)) * lon_count
    turns = phase * (1.0 / lon_count)
    cosine = turn_sine(jnp.abs(turns - 0.5) - 0.25)
    shifted = turns + 0.75
    shifted = jnp.where(shifted >= 1.0, shifted - 1.0, shifted)
    sine = turn_sine(jnp.abs(shifted - 0.5) - 0.25)
    return cosine, sine


def fill_table(orders_ref, table_ref, lon_count, degree_total, scale):
    bands, mine = orders_ref.shape
    steps = -(-lon_count // LANES)
    lane = lax.broadcasted_iota(jnp.int32, (bands, LANES), 1).astype(F32)
    for s in range(mine):
        order = orders_ref[:, s : s + 1].astype(F32)
        gain = jnp.where(order < degree_total, scale, 0.0)
        fc, fs = cosine_sine(jnp.broadcast_to(order, lane.shape), lane, lon_count)
        fc, fs = fc * gain, fs * gain
        cc, cs = cosine_sine(jnp.broadcast_to(order, lane.shape), lane * LANES, lon_count)
        low = 2 * s * bands
        for j in range(steps):
            width = min(LANES, lon_count - j * LANES)
            c, q = cc[:, j : j + 1], cs[:, j : j + 1]
            cosine = fc * c - fs * q
            sine = fs * c + fc * q
            span = slice(j * LANES, j * LANES + width)
            table_ref[low : low + bands, span] = cosine[:, :width].astype(BF)
            table_ref[low + bands : low + 2 * bands, span] = (-sine[:, :width]).astype(BF)


def analyse_kernel(orders_ref, field_ref, out_ref, table, rows, *, degree_total, lon_count):
    lat, chan, lon = field_ref.shape
    bands, mine = orders_ref.shape
    pieces = 2 * mine
    fill_table(orders_ref, table, lon_count, degree_total, 1.0 / math.sqrt(lon_count))
    for t in range(lat):
        got = lax.dot_general(
            table[...], field_ref[t], (((1,), (1,)), ((), ())), preferred_element_type=F32
        )
        for half in range(0, pieces, 4):
            line = jnp.concatenate(
                [got[j * bands : (j + 1) * bands] for j in range(half, half + 4)], 1
            )
            for q in range(4 * chan // LANES):
                tile = half * chan // LANES + q
                rows[tile, pl.ds(t, bands, lat), :] = line[:, q * LANES : (q + 1) * LANES]
    for q in range(rows.shape[0]):
        out_ref[:, q * LANES : (q + 1) * LANES] = rows[q].astype(BF)


def analyse(orders, field, degree_total):
    lat, chan, lon = field.shape
    bands, mine = orders.shape
    return pl.pallas_call(
        functools.partial(analyse_kernel, degree_total=degree_total, lon_count=lon),
        out_shape=jax.ShapeDtypeStruct((bands * lat, 2 * mine * chan), BF),
        scratch_shapes=[
            pltpu.VMEM((2 * mine * bands, lon), BF),
            pltpu.VMEM((2 * mine * chan // LANES, bands * lat, LANES), F32),
        ],
        name="analyse",
    )(orders, field)


def table_kernel(orders_ref, out_ref, *, degree_total, lon_count):
    fill_table(orders_ref, out_ref, lon_count, degree_total, 1.0 / math.sqrt(degree_total))


def inverse_table(orders, lon_count, degree_total):
    bands, mine = orders.shape
    return pl.pallas_call(
        functools.partial(table_kernel, degree_total=degree_total, lon_count=lon_count),
        out_shape=jax.ShapeDtypeStruct((2 * mine * bands, lon_count), BF),
        name="inverse_table",
    )(orders)


def legendre_kernel(mine_ref, x_ref, a_ref, s_ref, filter_ref, out_ref):
    chan = filter_ref.shape[1]
    degree = lax.broadcasted_iota(jnp.int32, filter_ref.shape, 0)
    outs = []
    for h in range(2):
        order = mine_ref[2 * pl.program_id(0) + h]
        gain = jnp.where(degree >= order, filter_ref[...], 0.0)
        gain = jnp.concatenate([gain, gain], 1)
        x = x_ref[:, 2 * chan * h : 2 * chan * (h + 1)]
        coeffs = jnp.dot(a_ref[h], x, preferred_element_type=F32)
        scaled = (coeffs * gain).astype(BF)
        outs.append(
            lax.dot_general(s_ref[h], scaled, (((0,), (0,)), ((), ())), preferred_element_type=F32)
        )
    out_ref[...] = jnp.concatenate(outs, 1).astype(BF)


def legendre(mine, x, a, s, filters):
    slots, degrees, lat_all = a.shape
    chan = filters.shape[1]
    step = 2
    wide = pl.BlockSpec((lat_all, step * 2 * chan), lambda i, m: (0, i))
    table = pl.BlockSpec((step, degrees, lat_all), lambda i, m: (i, 0, 0))
    return pl.pallas_call(
        legendre_kernel,
        grid_spec=pltpu.PrefetchScalarGridSpec(
            num_scalar_prefetch=1,
            grid=(slots // step,),
            in_specs=[wide, table, table, pl.BlockSpec((degrees, chan), lambda i, m: (0, 0))],
            out_specs=wide,
        ),
        out_shape=jax.ShapeDtypeStruct(x.shape, BF),
        name="legendre",
    )(mine, x, a, s, filters)


def synth_kernel(table_ref, x_ref, field_ref, out_ref, rows, cols):
    lat, chan, lon = field_ref.shape
    pieces = x_ref.shape[1] // chan
    bands = x_ref.shape[0] // lat
    tiles = rows.shape[0]
    for q in range(tiles):
        rows[q] = x_ref[:, q * LANES : (q + 1) * LANES].astype(F32)
    for t in range(lat):
        line = jnp.concatenate([rows[q, pl.ds(t, bands, lat), :] for q in range(tiles)], 1).astype(BF)
        for j in range(pieces):
            cols[j * bands : (j + 1) * bands, :] = line[:, j * chan : (j + 1) * chan]
        total = lax.dot_general(
            cols[...], table_ref[...], (((0,), (0,)), ((), ())), preferred_element_type=F32
        )
        out_ref[t] = (field_ref[t].astype(F32) + total).astype(BF)


def synthesise(table, x, field):
    lat, chan, lon = field.shape
    return pl.pallas_call(
        synth_kernel,
        out_shape=jax.ShapeDtypeStruct(field.shape, BF),
        scratch_shapes=[
            pltpu.VMEM((x.shape[1] // LANES, x.shape[0], LANES), F32),
            pltpu.VMEM((table.shape[0], chan), BF),
        ],
        name="synthesise",
    )(table, x, field)


def crps_kernel(own_ref, a_ref, b_ref, c_ref, seen_ref, out_ref):
    own = own_ref[...].astype(F32)

    def slope(other):
        d = own - other.astype(F32)
        return d * lax.rsqrt(d * d + smooth_sq)

    pair = slope(a_ref[...]) + slope(b_ref[...]) + slope(c_ref[...])
    out_ref[...] = (slope(seen_ref[...]) - pair * (1.0 / ENS)).astype(BF)


def crps(own, a, b, c, seen):
    lat, chan, lon = own.shape
    spec = pl.BlockSpec((1, chan, lon), lambda t: (t, 0, 0))
    return pl.pallas_call(
        crps_kernel,
        grid=(lat,),
        in_specs=[spec] * 5,
        out_specs=spec,
        out_shape=jax.ShapeDtypeStruct(own.shape, BF),
        name="crps",
    )(own, a, b, c, seen)


def body(field, target, slot_orders, analysis, synthesis, degree_filter):
    lat, chan, lon = field.shape[1:]
    mine_count, degrees = analysis.shape[0], analysis.shape[2]
    bands = lax.axis_size("polar")
    ens = lax.axis_size("ens")
    width = 2 * mine_count * chan
    packed = (bands, lat // 2, 2, width)
    orders = slot_orders.reshape(bands, mine_count)
    spectral = analyse(orders, field[0], degrees).reshape(packed)
    got = lax.all_to_all(spectral, "polar", split_axis=0, concat_axis=0, tiled=True)
    inverse = inverse_table(orders, lon, degrees)
    group = lax.axis_index("ens") // ENS
    pick = (group * chan + jnp.arange(chan)[:, None] == jnp.arange(target.shape[1])[None, :]).astype(BF)
    seen = jnp.einsum("qc,tck->tqk", pick, target, preferred_element_type=F32).astype(BF)
    mine = lax.dynamic_slice_in_dim(slot_orders, lax.axis_index("polar") * mine_count, mine_count)
    filters = lax.dynamic_slice_in_dim(degree_filter.T, group * chan, chan, 1)
    out = legendre(
        mine, got.reshape(bands * lat, width), jnp.swapaxes(analysis, 1, 2), synthesis, filters
    )
    back = lax.all_to_all(out.reshape(packed), "polar", split_axis=0, concat_axis=0, tiled=True)
    prediction = synthesise(inverse, back.reshape(bands * lat, width), field[0])
    across = [(i, i ^ 2) for i in range(ens)]
    beside = [(i, i ^ 1) for i in range(ens)]
    parts = []
    half = lat // 2
    for h in range(2):
        own = prediction[h * half : (h + 1) * half]
        far = lax.ppermute(own, "ens", across)
        near = lax.ppermute(own, "ens", beside)
        far_near = lax.ppermute(far, "ens", beside)
        parts.append(crps(own, near, far, far_near, seen[h * half : (h + 1) * half]))
    gradient = jnp.concatenate(parts, 0)
    return prediction[None], gradient[None]


def solution(mesh):
    in_specs = (
        P("ens", "polar", None, None),
        P("polar", None, None),
        P(),
        P("polar", None, None),
        P("polar", None, None),
        P(),
    )
    out_specs = (P("ens", "polar", None, None), P("ens", "polar", None, None))
    return jax.shard_map(body, mesh=mesh, in_specs=in_specs, out_specs=out_specs, check_vma=False)
```

time: 288 us -> 199 us (0.69)
  blocking collectives: 88.4 us -> 0 us
  local copies, waits for them, and re-layouts: 63.9 us -> 21.4 us
  other arithmetic: 32.5 us -> 2.15 us
  starting transfers between devices: 34.9 us -> 62.6 us
  Pallas kernels: 0 us -> 26.9 us
  waiting for transfers between devices: 58.4 us -> 82.9 us
  matrix products: 7.94 us -> 1.18 us
    all_to_all x2 -> x0, blocking collectives: 88.4 us -> none  [the longest x1 68.1 us: body(): lax.all_to_all(bands, 'polar', split_axis=2, concat_axis=0, tiled=True)]
    pallas_call x0 -> x6, Pallas kernels: none -> 26.9 us  [the longest x2 7.52 us: crps(): pl.pallas_call(crps_kernel, grid=(lat,), in_specs=[spec] * 5, out_specs=s...]
    ppermute x0 -> x6, starting transfers between devices: none -> 25.9 us  [the longest x2 11.6 us: body(): far_near = lax.ppermute(far, 'ens', beside)]
    all_to_all x2, waiting for transfers between devices: 58.4 us -> 82.9 us  [the longest x1 41.9 us: body(): lax.all_to_all(spectral, 'polar', split_axis=0, concat_axis=0, tiled=True)]
    add x4 -> x1, other arithmetic: 16.2 us -> 0.01 us  [body(): group * chan + jnp.arange(chan)[:, None]]
    unnamed x17 -> x10, local copies, waits for them, and re-layouts: 17.7 us -> 1.53 us
    convert_element_type x7 -> x0, local copies, waits for them, and re-layouts: 15.5 us -> none  [the longest x2 5.39 us: lon_tables(): forward = (paired / math.sqrt(lon_count)).astype(jnp.bfloat16)]
    convert_element_type x6 -> x0, other arithmetic: 8.48 us -> none  [the longest x1 2.52 us: crps_slope(): own_term = kernel_slope(values - observed.astype(jnp.float32)[:, None])]
  transfers between devices with their start and end apart: 2 -> 8, of which waited for: 2 -> 2; matrix products, arithmetic and copies ran while one was open for 5% -> 3% of each run, Pallas kernels for 0% -> 4%
where the time goes in v1:
time: 199 us; the launch traced here: 198 us
  waiting for transfers between devices  82.9 us (42%)
  starting transfers between devices  62.6 us (31%)
  Pallas kernels  26.9 us (14%)
  local copies, waits for them, and re-layouts  21.4 us (11%)
  other arithmetic  2.15 us (1%)
    all_to_all x1, waiting for transfers between devices, body(): lax.all_to_all(spectral, 'polar', split_axis=0, concat_axis=0, tiled=True)  41.9 us
    all_to_all x1, waiting for transfers between devices, body(): lax.all_to_all(out.reshape(packed), 'polar', split_axis=0, concat_axis=0,...  41 us
    all_to_all x1, starting transfers between devices, body(): lax.all_to_all(spectral, 'polar', split_axis=0, concat_axis=0, tiled=True)  25.8 us
    ppermute x2, starting transfers between devices, body(): far_near = lax.ppermute(far, 'ens', beside)  11.6 us
    all_to_all x1, starting transfers between devices, body(): lax.all_to_all(out.reshape(packed), 'polar', split_axis=0, concat_axis=0,...  11 us
    ppermute x2, starting transfers between devices, body(): near = lax.ppermute(own, 'ens', beside)  9 us
    pallas_call x2, Pallas kernels, crps(): pl.pallas_call(crps_kernel, grid=(lat,), in_specs=[spec] * 5, out_specs=s...  7.52 us
    pallas_call x1, Pallas kernels, legendre(): pl.pallas_call(legendre_kernel, grid_spec=pltpu.PrefetchScalarGridSpec(nu...  6.14 us
  transfers between devices with their start and end apart: 8, of which 2 were waited for; matrix products, arithmetic and copies ran while one was open for 3% of the time, Pallas kernels for 4%

profile of v1, /device:TPU:1, one launch (start us, length us, event | category | flops | bytes accessed | tf_op | source)
XLA Modules:
  0.0 198.0 jit_solution(10576283064917652388)
XLA Ops:
  0.6 0.0 copy-start
  0.6 1.6 reshape.24.orders_ref
  2.2 5.3 %analyse.1 = bf16[384,1152]{1,0:T(8,128)(2,1)} custom-call(s32[64,6]{1,0:T(8,128)} %reshape.24.orders_ref, bf16[6,96,720]{2,1,0:T(8,128)(2,1)} %bitcast.13), custom_call_target="tpu_custom_call" | custom-call | tf_op jit(solution)/shard_map/analyse/pallas_call | solution.py:82
  7.5 3.0 %reshape.25 = bf16[64,3,2,1152]{3,2,1,0:T(2,128)(2,1)} reshape(bf16[384,1152]{1,0:T(8,128)(2,1)} %analyse.1) | data formatting | bytes 1769472 | tf_op jit(solution)/shard_map/reshape | solution.py:204
  10.5 25.8 %all-to-all-start = ((bf16[64,3,2,1152]{3,2,1,0:T(2,128)(2,1)}), bf16[64,3,2,1152]{3,2,1,0:T(2,128)(2,1)}, u32[]{:S(2)}, u32[]{:S(2)}) async-start(bf16[64,3,2,1152]{3,2,1,0:T(2,128)(2,1)} %reshape.25), calls=%async_computation | async-start | bytes 1769472 | tf_op jit(solution)/shard_map/all_to_all | solution.py:205
  36.4 1.3 dynamic_slice.6.mine_ref
  37.6 1.8 dynamic-slice_bitcast_fusion.filter_ref
  39.4 41.9 %all-to-all-done = bf16[64,3,2,1152]{3,2,1,0:T(2,128)(2,1)} async-done(((bf16[64,3,2,1152]{3,2,1,0:T(2,128)(2,1)}), bf16[64,3,2,1152]{3,2,1,0:T(2,128)(2,1)}, u32[]{:S(2)}, u32[]{:S(2)}) %all-to-all-start) | async-done | bytes 884768 | tf_op jit(solution)/shard_map/all_to_all | solution.py:205
  81.4 3.1 %reshape.26.x_ref = bf16[384,1152]{1,0:T(8,128)(2,1)} reshape(bf16[64,3,2,1152]{3,2,1,0:T(2,128)(2,1)} %all-to-all-done) | data formatting | bytes 1769472 | tf_op jit(solution)/shard_map/reshape | solution.py:213
  84.5 6.1 %legendre.1 = bf16[384,1152]{1,0:T(8,128)(2,1)} custom-call(s32[6]{0:T(128)} %dynamic_slice.6.mine_ref, bf16[384,1152]{1,0:T(8,128)(2,1)} %reshape.26.x_ref, bf16[6,360,384]{2,1,0:T(8,128)(2,1)} %bitcast.16, bf16[6,360,384]{2,1,0:T(8,128)(2,1)} %s_ref.1, f32[360,96]{1,0:T(8,128)} %dynamic-slice_bitcast_fusion.filter_ref), custom_call_target="tpu_custom_call" | custom-call | tf_op jit(solution)/shard_map/legendre/pallas_call | solution.py:129
  90.6 3.0 %reshape.27 = bf16[64,3,2,1152]{3,2,1,0:T(2,128)(2,1)} reshape(bf16[384,1152]{1,0:T(8,128)(2,1)} %legendre.1) | data formatting | bytes 1769472 | tf_op jit(solution)/shard_map/reshape | solution.py:215
  93.6 11.0 %all-to-all-start.1 = ((bf16[64,3,2,1152]{3,2,1,0:T(2,128)(2,1)}), bf16[64,3,2,1152]{3,2,1,0:T(2,128)(2,1)}, u32[]{:S(2)}, u32[]{:S(2)}) async-start(bf16[64,3,2,1152]{3,2,1,0:T(2,128)(2,1)} %reshape.27), calls=%async_computation.1 | async-start | bytes 1769472 | tf_op jit(solution)/shard_map/all_to_all | solution.py:215
  104.6 3.3 %inverse_table.1.table_ref = bf16[768,720]{1,0:T(8,128)(2,1)} custom-call(s32[64,6]{1,0:T(8,128)} %reshape.24.orders_ref), custom_call_target="tpu_custom_call" | custom-call | tf_op jit(solution)/shard_map/inverse_table/pallas_call | solution.py:99
  107.9 41.0 %all-to-all-done.1 = bf16[64,3,2,1152]{3,2,1,0:T(2,128)(2,1)} async-done(((bf16[64,3,2,1152]{3,2,1,0:T(2,128)(2,1)}), bf16[64,3,2,1152]{3,2,1,0:T(2,128)(2,1)}, u32[]{:S(2)}, u32[]{:S(2)}) %all-to-all-start.1) | async-done | bytes 884768 | tf_op jit(solution)/shard_map/all_to_all | solution.py:215
  148.9 3.1 %reshape.28.x_ref = bf16[384,1152]{1,0:T(8,128)(2,1)} reshape(bf16[64,3,2,1152]{3,2,1,0:T(2,128)(2,1)} %all-to-all-done.1) | data formatting | bytes 1769472 | tf_op jit(solution)/shard_map/reshape | solution.py:216
  152.1 4.6 %synthesise.1 = bf16[6,96,720]{2,1,0:T(8,128)(2,1)} custom-call(bf16[768,720]{1,0:T(8,128)(2,1)} %inverse_table.1.table_ref, bf16[384,1152]{1,0:T(8,128)(2,1)} %reshape.28.x_ref, bf16[6,96,720]{2,1,0:T(8,128)(2,1)} %bitcast.14), custom_call_target="tpu_custom_call" | custom-call | tf_op jit(solution)/shard_map/synthesise/pallas_call | solution.py:161
  156.7 2.0 fusion.5
  158.7 3.1 %collective-permute-start.1 = (bf16[3,96,720]{2,1,0:T(8,128)(2,1)S(1)}, bf16[3,96,720]{2,1,0:T(8,128)(2,1)S(1)}, u32[]{:S(2)}, u32[]{:S(2)}) collective-permute-start(bf16[3,96,720]{2,1,0:T(8,128)(2,1)S(1)} %get-tuple-element.4.own_ref), channel_id=1, source_target_pairs={{0,128},{64,192},{128,0},{192,64},{256,384},{320,448},{384,256},{4... | collective-permute-start | bytes 1244168 | tf_op jit(solution)/shard_map/ppermute | solution.py:223
  161.8 2.2 %collective-permute-start.4 = (bf16[3,96,720]{2,1,0:T(8,128)(2,1)}, bf16[3,96,720]{2,1,0:T(8,128)(2,1)}, u32[]{:S(2)}, u32[]{:S(2)}) collective-permute-start(bf16[3,96,720]{2,1,0:T(8,128)(2,1)} %get-tuple-element.5.own_ref), channel_id=1, source_target_pairs={{0,128},{64,192},{128,0},{192,64},{256,384},{320,448},{384,256},{4... | collective-permute-start | bytes 1244168 | tf_op jit(solution)/shard_map/ppermute | solution.py:223
  164.0 7.1 %collective-permute-start = (bf16[3,96,720]{2,1,0:T(8,128)(2,1)S(1)}, bf16[3,96,720]{2,1,0:T(8,128)(2,1)S(1)}, u32[]{:S(2)}, u32[]{:S(2)}) collective-permute-start(bf16[3,96,720]{2,1,0:T(8,128)(2,1)S(1)} %get-tuple-element.4.own_ref), channel_id=1, source_target_pairs={{0,64},{64,0},{128,192},{192,128},{256,320},{320,256},{384,448},{4... | collective-permute-start | bytes 1244168 | tf_op jit(solution)/shard_map/ppermute | solution.py:224
  171.0 1.9 collective-permute-start.3
  173.0 0.0 collective-permute-done.1.b_ref
  173.0 6.8 %collective-permute-start.2 = (bf16[3,96,720]{2,1,0:T(8,128)(2,1)S(1)}, bf16[3,96,720]{2,1,0:T(8,128)(2,1)S(1)}, u32[]{:S(2)}, u32[]{:S(2)}) collective-permute-start(bf16[3,96,720]{2,1,0:T(8,128)(2,1)S(1)} %collective-permute-done.1.b_ref), channel_id=1, source_target_pairs={{0,64},{64,0},{128,192},{192,128},{256,320},{320,256},{384,448},{4... | collective-permute-start | bytes 1244168 | tf_op jit(solution)/shard_map/ppermute | solution.py:225
  179.8 0.0 collective-permute-done.4.b_ref
  179.8 4.8 %collective-permute-start.5 = (bf16[3,96,720]{2,1,0:T(8,128)(2,1)}, bf16[3,96,720]{2,1,0:T(8,128)(2,1)}, u32[]{:S(2)}, u32[]{:S(2)}) collective-permute-start(bf16[3,96,720]{2,1,0:T(8,128)(2,1)} %collective-permute-done.4.b_ref), channel_id=1, source_target_pairs={{0,64},{64,0},{128,192},{192,128},{256,320},{320,256},{384,448},{4... | collective-permute-start | bytes 1244168 | tf_op jit(solution)/shard_map/ppermute | solution.py:225
  184.6 1.2 fusion
  185.8 1.0 fusion.4
  186.8 0.7 copy-done.3
  187.6 0.8 copy-done.4
  188.3 3.7 %crps.2 = bf16[3,96,720]{2,1,0:T(8,128)(2,1)} custom-call(bf16[3,96,720]{2,1,0:T(8,128)(2,1)} %copy-done.1, bf16[3,96,720]{2,1,0:T(8,128)(2,1)} %copy-done.3, bf16[3,96,720]{2,1,0:T(8,128)(2,1)} %copy-done.2, bf16[3,96,720]{2,1,0:T(8,128)(2,1)} %copy-done.4, bf16[3,96,720]{2,1,0:T(8,128)(2,1)} %get-tuple-element.2.seen_ref), custom_call_target="tpu_custom_call" | custom-call | tf_op jit(solution)/shard_map/crps/pallas_call | solution.py:186
  192.1 3.8 %crps.3 = bf16[3,96,720]{2,1,0:T(8,128)(2,1)} custom-call(bf16[3,96,720]{2,1,0:T(8,128)(2,1)} %get-tuple-element.5.own_ref, bf16[3,96,720]{2,1,0:T(8,128)(2,1)} %collective-permute-done.3.a_ref, bf16[3,96,720]{2,1,0:T(8,128)(2,1)} %collective-permute-done.4.b_ref, bf16[3,96,720]{2,1,0:T(8,128)(2,1)} %collective-permute-done.5.c_ref, ...), custom_call_target="tpu_custom_call" | custom-call | tf_op jit(solution)/shard_map/crps/pallas_call | solution.py:186
  195.9 2.1 %maximum_bitcast_fusion = bf16[1,6,96,720]{3,2,1,0:T(8,128)(2,1)} fusion(bf16[3,96,720]{2,1,0:T(8,128)(2,1)} %crps.3, bf16[3,96,720]{2,1,0:T(8,128)(2,1)} %crps.2), kind=kLoop, calls=%fused_computation.2 | loop fusion | flops 414720 | bytes 1658880 | tf_op jit(solution)/shard_map/broadcast_in_dim | solution.py:228
  (12 shorter events, 0.0 us)
Async XLA Ops:
  0.6 184.0 %copy-start = (bf16[6,384,720]{1,2,0:T(8,128)(2,1)S(1)}, bf16[6,384,720]{1,2,0:T(8,128)(2,1)}, u32[]{:S(2)}) copy-start(bf16[6,384,720]{1,2,0:T(8,128)(2,1)} %param.7) | copy-start | bytes 9953284
  10.5 70.8 %all-to-all-start = ((bf16[64,3,2,1152]{3,2,1,0:T(2,128)(2,1)}), bf16[64,3,2,1152]{3,2,1,0:T(2,128)(2,1)}, u32[]{:S(2)}, u32[]{:S(2)}) async-start(bf16[64,3,2,1152]{3,2,1,0:T(2,128)(2,1)} %reshape.25), calls=%async_computation | async-start | bytes 1769472 | tf_op jit(solution)/shard_map/all_to_all | solution.py:205
  93.6 55.3 %all-to-all-start.1 = ((bf16[64,3,2,1152]{3,2,1,0:T(2,128)(2,1)}), bf16[64,3,2,1152]{3,2,1,0:T(2,128)(2,1)}, u32[]{:S(2)}, u32[]{:S(2)}) async-start(bf16[64,3,2,1152]{3,2,1,0:T(2,128)(2,1)} %reshape.27), calls=%async_computation.1 | async-start | bytes 1769472 | tf_op jit(solution)/shard_map/all_to_all | solution.py:215
  158.7 28.1 %copy-start.1 = (bf16[3,96,720]{2,1,0:T(8,128)(2,1)}, bf16[3,96,720]{2,1,0:T(8,128)(2,1)S(1)}, u32[]{:S(2)}) copy-start(bf16[3,96,720]{2,1,0:T(8,128)(2,1)S(1)} %get-tuple-element.4.own_ref) | copy-start | bytes 1244164
  158.7 14.3 %collective-permute-start.1 = (bf16[3,96,720]{2,1,0:T(8,128)(2,1)S(1)}, bf16[3,96,720]{2,1,0:T(8,128)(2,1)S(1)}, u32[]{:S(2)}, u32[]{:S(2)}) collective-permute-start(bf16[3,96,720]{2,1,0:T(8,128)(2,1)S(1)} %get-tuple-element.4.own_ref), channel_id=1, source_target_pairs={{0,128},{64,192},{128,0},{192,64},{256,384},{320,448},{384,256},{4... | collective-permute-start | bytes 1244168 | tf_op jit(solution)/shard_map/ppermute | solution.py:223
  161.8 18.0 %collective-permute-start.4 = (bf16[3,96,720]{2,1,0:T(8,128)(2,1)}, bf16[3,96,720]{2,1,0:T(8,128)(2,1)}, u32[]{:S(2)}, u32[]{:S(2)}) collective-permute-start(bf16[3,96,720]{2,1,0:T(8,128)(2,1)} %get-tuple-element.5.own_ref), channel_id=1, source_target_pairs={{0,128},{64,192},{128,0},{192,64},{256,384},{320,448},{384,256},{4... | collective-permute-start | bytes 1244168 | tf_op jit(solution)/shard_map/ppermute | solution.py:223
  164.0 22.8 %collective-permute-start = (bf16[3,96,720]{2,1,0:T(8,128)(2,1)S(1)}, bf16[3,96,720]{2,1,0:T(8,128)(2,1)S(1)}, u32[]{:S(2)}, u32[]{:S(2)}) collective-permute-start(bf16[3,96,720]{2,1,0:T(8,128)(2,1)S(1)} %get-tuple-element.4.own_ref), channel_id=1, source_target_pairs={{0,64},{64,0},{128,192},{192,128},{256,320},{320,256},{384,448},{4... | collective-permute-start | bytes 1244168 | tf_op jit(solution)/shard_map/ppermute | solution.py:224
  171.0 21.0 %collective-permute-start.3 = (bf16[3,96,720]{2,1,0:T(8,128)(2,1)}, bf16[3,96,720]{2,1,0:T(8,128)(2,1)}, u32[]{:S(2)}, u32[]{:S(2)}) collective-permute-start(bf16[3,96,720]{2,1,0:T(8,128)(2,1)} %get-tuple-element.5.own_ref), channel_id=1, source_target_pairs={{0,64},{64,0},{128,192},{192,128},{256,320},{320,256},{384,448},{4... | collective-permute-start | bytes 1244168 | tf_op jit(solution)/shard_map/ppermute | solution.py:224
  173.0 13.8 %copy-start.2 = (bf16[3,96,720]{2,1,0:T(8,128)(2,1)}, bf16[3,96,720]{2,1,0:T(8,128)(2,1)S(1)}, u32[]{:S(2)}) copy-start(bf16[3,96,720]{2,1,0:T(8,128)(2,1)S(1)} %collective-permute-done.1.b_ref) | copy-start | bytes 1244164
  173.0 13.8 %collective-permute-start.2 = (bf16[3,96,720]{2,1,0:T(8,128)(2,1)S(1)}, bf16[3,96,720]{2,1,0:T(8,128)(2,1)S(1)}, u32[]{:S(2)}, u32[]{:S(2)}) collective-permute-start(bf16[3,96,720]{2,1,0:T(8,128)(2,1)S(1)} %collective-permute-done.1.b_ref), channel_id=1, source_target_pairs={{0,64},{64,0},{128,192},{192,128},{256,320},{320,256},{384,448},{4... | collective-permute-start | bytes 1244168 | tf_op jit(solution)/shard_map/ppermute | solution.py:225
  179.8 12.3 %collective-permute-start.5 = (bf16[3,96,720]{2,1,0:T(8,128)(2,1)}, bf16[3,96,720]{2,1,0:T(8,128)(2,1)}, u32[]{:S(2)}, u32[]{:S(2)}) collective-permute-start(bf16[3,96,720]{2,1,0:T(8,128)(2,1)} %collective-permute-done.4.b_ref), channel_id=1, source_target_pairs={{0,64},{64,0},{128,192},{192,128},{256,320},{320,256},{384,448},{4... | collective-permute-start | bytes 1244168 | tf_op jit(solution)/shard_map/ppermute | solution.py:225
  186.8 0.8 copy-start.3
  187.6 0.8 copy-start.4

commit v2 on v1

v2 whole, which is shorter than its diff:
```python
import functools
import math

import jax
import jax.numpy as jnp
from jax import lax
from jax.experimental import pallas as pl
from jax.experimental.pallas import tpu as pltpu
from jax.sharding import PartitionSpec as P

ENS = 4
BF = jnp.bfloat16
F32 = jnp.float32
smooth_sq = 0.25
LANES = 128
GROUP = 2


def turn_sine(turns):
    w = turns * (2.0 * math.pi)
    w2 = w * w
    poly = -2.5052108e-8 + w2 * 1.6059044e-10
    for coef in (2.7557319e-6, -1.9841270e-4, 8.3333333e-3, -1.6666667e-1, 1.0):
        poly = poly * w2 + coef
    return poly * w


def cosine_sine(orders, points, lon_count):
    product = orders * points
    phase = product - jnp.floor(product * (1.0 / lon_count)) * lon_count
    turns = phase * (1.0 / lon_count)
    cosine = turn_sine(jnp.abs(turns - 0.5) - 0.25)
    shifted = turns + 0.75
    shifted = jnp.where(shifted >= 1.0, shifted - 1.0, shifted)
    sine = turn_sine(jnp.abs(shifted - 0.5) - 0.25)
    return cosine, sine


def fill_table(orders_ref, table_ref, bands, lon_count, degree_total, scale):
    slots = orders_ref.shape[1]
    mine = slots // bands
    shape = (bands, LANES)
    lane = lax.broadcasted_iota(jnp.int32, shape, 1).astype(F32)
    every = orders_ref[...].astype(F32)
    first = mine * lax.broadcasted_iota(jnp.int32, (bands, slots), 0)
    place = lax.broadcasted_iota(jnp.int32, (bands, slots), 1)
    for s in range(mine):
        order = jnp.sum(jnp.where(place == first + s, every, 0.0), 1, keepdims=True)
        order = jnp.broadcast_to(order, shape)
        gain = jnp.where(order < degree_total, scale, 0.0)
        cosine, sine = cosine_sine(order, lane, lon_count)
        cosine, sine = cosine * gain, sine * gain
        turn_c, turn_s = cosine_sine(order, float(LANES), lon_count)
        low = 2 * s * bands
        for start in range(0, lon_count, LANES):
            width = min(LANES, lon_count - start)
            span = slice(start, start + width)
            table_ref[low : low + bands, span] = cosine[:, :width].astype(BF)
            table_ref[low + bands : low + 2 * bands, span] = (-sine[:, :width]).astype(BF)
            cosine, sine = cosine * turn_c - sine * turn_s, sine * turn_c + cosine * turn_s


def analyse_kernel(orders_ref, field_ref, out_ref, table, rows, *, bands, degree_total):
    lat, chan, lon = field_ref.shape
    pieces = table.shape[0] // bands
    fill_table(orders_ref, table, bands, lon, degree_total, 1.0 / math.sqrt(lon))
    group = GROUP
    for t0 in range(0, lat, group):
        got = lax.dot_general(
            table[...],
            field_ref[t0 : t0 + group].reshape(group * chan, lon),
            (((1,), (1,)), ((), ())),
            preferred_element_type=F32,
        )
        for u in range(group):
            for start in range(0, pieces, 4):
                line = jnp.concatenate(
                    [
                        got[j * bands : (j + 1) * bands, u * chan : (u + 1) * chan]
                        for j in range(start, start + 4)
                    ],
                    1,
                )
                for q in range(4 * chan // LANES):
                    tile = start * chan // LANES + q
                    rows[tile, pl.ds(t0 + u, bands, lat), :] = line[:, q * LANES : (q + 1) * LANES]
    for q in range(rows.shape[0]):
        packed = rows[q].astype(BF).reshape(out_ref.shape[0], 2, LANES)
        out_ref[:, :, q * LANES : (q + 1) * LANES] = packed


def analyse(orders, field, bands, degree_total):
    lat, chan, lon = field.shape
    pieces = 2 * orders.shape[1] // bands
    return pl.pallas_call(
        functools.partial(analyse_kernel, bands=bands, degree_total=degree_total),
        out_shape=jax.ShapeDtypeStruct((bands * lat // 2, 2, pieces * chan), BF),
        scratch_shapes=[
            pltpu.VMEM((pieces * bands, lon), BF),
            pltpu.VMEM((pieces * chan // LANES, bands * lat, LANES), F32),
        ],
        name="analyse",
    )(orders, field)


def table_kernel(orders_ref, out_ref, *, bands, degree_total):
    scale = 1.0 / math.sqrt(degree_total)
    fill_table(orders_ref, out_ref, bands, out_ref.shape[1], degree_total, scale)


def inverse_table(orders, bands, lon_count, degree_total):
    return pl.pallas_call(
        functools.partial(table_kernel, bands=bands, degree_total=degree_total),
        out_shape=jax.ShapeDtypeStruct((2 * orders.shape[1], lon_count), BF),
        name="inverse_table",
    )(orders)


def legendre_kernel(mine_ref, x_ref, a_ref, s_ref, filter_ref, out_ref):
    chan = filter_ref.shape[1]
    lat_all = a_ref.shape[2]
    degree = lax.broadcasted_iota(jnp.int32, filter_ref.shape, 0)
    both = x_ref[...].reshape(lat_all, x_ref.shape[2])
    outs = []
    for h in range(2):
        order = mine_ref[2 * pl.program_id(0) + h]
        gain = jnp.where(degree >= order, filter_ref[...], 0.0)
        gain = jnp.concatenate([gain, gain], 1)
        x = both[:, 2 * chan * h : 2 * chan * (h + 1)]
        coeffs = jnp.dot(a_ref[h], x, preferred_element_type=F32)
        scaled = (coeffs * gain).astype(BF)
        outs.append(jnp.dot(s_ref[h], scaled, preferred_element_type=F32))
    out_ref[...] = jnp.concatenate(outs, 1).astype(BF).reshape(out_ref.shape)


def legendre(mine, x, a, s, filters):
    slots, degrees, lat_all = a.shape
    chan = filters.shape[1]
    step = 2
    wide = pl.BlockSpec((lat_all // 2, 2, step * 2 * chan), lambda i, m: (0, 0, i))
    return pl.pallas_call(
        legendre_kernel,
        grid_spec=pltpu.PrefetchScalarGridSpec(
            num_scalar_prefetch=1,
            grid=(slots // step,),
            in_specs=[
                wide,
                pl.BlockSpec((step, degrees, lat_all), lambda i, m: (i, 0, 0)),
                pl.BlockSpec((step, lat_all, degrees), lambda i, m: (i, 0, 0)),
                pl.BlockSpec((degrees, chan), lambda i, m: (0, 0)),
            ],
            out_specs=wide,
        ),
        out_shape=jax.ShapeDtypeStruct(x.shape, BF),
        name="legendre",
    )(mine, x, a, s, filters)


def synth_kernel(table_ref, x_ref, field_ref, out_ref, low_ref, high_ref, rows, cols):
    lat, chan, lon = field_ref.shape
    pieces = x_ref.shape[2] // chan
    bands = table_ref.shape[0] // pieces
    tiles = rows.shape[0]
    first = low_ref.shape[0]
    for q in range(tiles):
        rows[q] = x_ref[:, :, q * LANES : (q + 1) * LANES].reshape(lat * bands, LANES).astype(F32)
    for t in range(lat):
        line = jnp.concatenate([rows[q, pl.ds(t, bands, lat), :] for q in range(tiles)], 1).astype(BF)
        for j in range(pieces):
            cols[j * bands : (j + 1) * bands, :] = line[:, j * chan : (j + 1) * chan]
        total = lax.dot_general(
            cols[...], table_ref[...], (((0,), (0,)), ((), ())), preferred_element_type=F32
        )
        done = (field_ref[t].astype(F32) + total).astype(BF)
        out_ref[t] = done
        if t < first:
            low_ref[t] = done
        else:
            high_ref[t - first] = done


def synthesise(table, x, field, first):
    lat, chan, lon = field.shape
    tiles = x.shape[2] // LANES
    return pl.pallas_call(
        synth_kernel,
        out_shape=[
            jax.ShapeDtypeStruct((n, chan, lon), BF) for n in (lat, first, lat - first)
        ],
        scratch_shapes=[
            pltpu.VMEM((tiles, x.shape[0] * 2, LANES), F32),
            pltpu.VMEM((table.shape[0], chan), BF),
        ],
        name="synthesise",
    )(table, x, field)


def crps_kernel(own_ref, near_ref, far_ref, far_near_ref, seen_ref, *rest):
    out_ref = rest[-1]
    own = own_ref[...].astype(F32)

    def slope(other):
        d = own - other[...].astype(F32)
        return d * lax.rsqrt(d * d + smooth_sq)

    pair = slope(near_ref) + slope(far_ref) + slope(far_near_ref)
    out_ref[...] = (slope(seen_ref) - pair * (1.0 / ENS)).astype(BF)


def crps(own, near, far, far_near, seen, start, filled=None):
    lat, chan, lon = near.shape
    part = pl.BlockSpec((1, chan, lon), lambda t: (t, 0, 0))
    whole = pl.BlockSpec((1, chan, lon), lambda t: (t + start, 0, 0))
    more = [] if filled is None else [filled]
    return pl.pallas_call(
        crps_kernel,
        grid=(lat,),
        in_specs=[whole, part, part, part, whole] + [pl.BlockSpec(memory_space=pl.ANY)] * len(more),
        out_specs=whole,
        out_shape=jax.ShapeDtypeStruct(own.shape, BF),
        input_output_aliases={5: 0} if more else {},
        name="crps",
    )(own, near, far, far_near, seen, *more)


def body(field, target, slot_orders, analysis, synthesis, degree_filter):
    lat, chan, lon = field.shape[1:]
    mine_count, degrees = analysis.shape[0], analysis.shape[2]
    bands = lax.axis_size("polar")
    ens = lax.axis_size("ens")
    width = 2 * mine_count * chan
    packed = (bands, lat // 2, 2, width)
    flat = (bands * lat // 2, 2, width)
    orders = slot_orders.reshape(1, bands * mine_count)
    spectral = analyse(orders, field[0], bands, degrees).reshape(packed)
    got = lax.all_to_all(spectral, "polar", split_axis=0, concat_axis=0, tiled=True)
    group = lax.axis_index("ens") // ENS
    mine = lax.dynamic_slice_in_dim(slot_orders, lax.axis_index("polar") * mine_count, mine_count)
    filters = lax.dynamic_slice_in_dim(degree_filter.T, group * chan, chan, 1)
    turned = jnp.swapaxes(synthesis, 1, 2)
    got, turned, filters = lax.optimization_barrier((got, turned, filters))
    out = legendre(mine, got.reshape(flat), jnp.swapaxes(analysis, 1, 2), turned, filters)
    back = lax.all_to_all(out.reshape(packed), "polar", split_axis=0, concat_axis=0, tiled=True)
    inverse = inverse_table(orders, bands, lon, degrees)
    pick = (group * chan + jnp.arange(chan)[:, None] == jnp.arange(target.shape[1])[None, :]).astype(BF)
    seen = jnp.einsum("qc,tck->tqk", pick, target, preferred_element_type=F32).astype(BF)
    back, inverse, seen = lax.optimization_barrier((back, inverse, seen))
    first = 4
    prediction, low, high = synthesise(inverse, back.reshape(flat), field[0], first)
    across = [(i, i ^ 2) for i in range(ens)]
    beside = [(i, i ^ 1) for i in range(ens)]
    gradient = None
    for start, own in ((0, low), (first, high)):
        far = lax.ppermute(own, "ens", across)
        near = lax.ppermute(own, "ens", beside)
        far_near = lax.ppermute(far, "ens", beside)
        gradient = crps(prediction, near, far, far_near, seen, start, gradient)
    return prediction[None], gradient[None]


def solution(mesh):
    in_specs = (
        P("ens", "polar", None, None),
        P("polar", None, None),
        P(),
        P("polar", None, None),
        P("polar", None, None),
        P(),
    )
    out_specs = (P("ens", "polar", None, None), P("ens", "polar", None, None))
    return jax.shard_map(body, mesh=mesh, in_specs=in_specs, out_specs=out_specs, check_vma=False)
```

time: 199 us -> 188 us (0.945)
  local copies, waits for them, and re-layouts: 21.4 us -> 10.8 us
  waiting for transfers between devices: 82.9 us -> 85.9 us
  other arithmetic: 2.15 us -> 0.01 us
    reshape x5 -> x1, local copies, waits for them, and re-layouts: 13.9 us -> 1.43 us  [body(): orders = slot_orders.reshape(1, bands * mine_count)]
    ppermute x2, waiting for transfers between devices: 0.01 us -> 8.03 us  [body(): far = lax.ppermute(own, 'ens', across)]
    unnamed x10 -> x9, local copies, waits for them, and re-layouts: 1.53 us -> 6.3 us
    all_to_all x1, waiting for transfers between devices: 41.9 us -> 38.2 us  [body(): lax.all_to_all(spectral, 'polar', split_axis=0, concat_axis=0, tiled=True)]
    slice x2 -> x0, local copies, waits for them, and re-layouts: 2.95 us -> none  [the longest x1 1.96 us: body(): own = prediction[h * half:(h + 1) * half]]
    broadcast_in_dim x1 -> x0, other arithmetic: 2.14 us -> none  [body(): return (prediction[None], gradient[None])]
  transfers between devices with their start and end apart: 8 -> 8, of which waited for: 2 -> 4; matrix products, arithmetic and copies ran while one was open for 3% -> 5% of each run, Pallas kernels for 4% -> 4%
where the time goes in v2:
time: 188 us; the launch traced here: 187 us
  waiting for transfers between devices  85.9 us (46%)
  starting transfers between devices  61.8 us (33%)
  Pallas kernels  25.5 us (14%)
  local copies, waits for them, and re-layouts  10.8 us (6%)
  matrix products  2.1 us (1%)
    all_to_all x1, waiting for transfers between devices, body(): lax.all_to_all(out.reshape(packed), 'polar', split_axis=0, concat_axis=0,...  39.7 us
    all_to_all x1, waiting for transfers between devices, body(): lax.all_to_all(spectral, 'polar', split_axis=0, concat_axis=0, tiled=True)  38.2 us
    all_to_all x1, starting transfers between devices, body(): lax.all_to_all(spectral, 'polar', split_axis=0, concat_axis=0, tiled=True)  25.8 us
    all_to_all x1, starting transfers between devices, body(): lax.all_to_all(out.reshape(packed), 'polar', split_axis=0, concat_axis=0,...  10.8 us
    ppermute x2, starting transfers between devices, body(): far_near = lax.ppermute(far, 'ens', beside)  10.1 us
    ppermute x2, starting transfers between devices, body(): near = lax.ppermute(own, 'ens', beside)  8.92 us
    ppermute x2, waiting for transfers between devices, body(): far = lax.ppermute(own, 'ens', across)  8.03 us
    pallas_call x2, Pallas kernels, crps(): pl.pallas_call(crps_kernel, grid=(lat,), in_specs=[whole, part, part, par...  6.77 us
  transfers between devices with their start and end apart: 8, of which 4 were waited for; matrix products, arithmetic and copies ran while one was open for 5% of the time, Pallas kernels for 4%

profile of v2, /device:TPU:1, one launch (start us, length us, event | category | flops | bytes accessed | tf_op | source)
XLA Modules:
  0.0 186.7 jit_solution(12132967926859656223)
XLA Ops:
  0.6 0.0 copy-start
  0.6 1.4 reshape.24.orders_ref
  2.1 4.6 %analyse.1 = bf16[192,2,1152]{2,1,0:T(2,128)(2,1)} custom-call(s32[1,384]{1,0:T(1,128)} %reshape.24.orders_ref, bf16[6,96,720]{2,1,0:T(8,128)(2,1)} %bitcast.18), custom_call_target="tpu_custom_call" | custom-call | tf_op jit(solution)/shard_map/analyse/pallas_call | solution.py:95
  6.7 25.8 %all-to-all-start = ((bf16[64,3,2,1152]{3,2,1,0:T(2,128)(2,1)}), bf16[64,3,2,1152]{3,2,1,0:T(2,128)(2,1)}, u32[]{:S(2)}, u32[]{:S(2)}) async-start(bf16[64,3,2,1152]{3,2,1,0:T(2,128)(2,1)} %bitcast.20), calls=%async_computation | async-start | bytes 1769472 | tf_op jit(solution)/shard_map/all_to_all | solution.py:236
  32.5 3.8 %copy.9 = bf16[6,360,384]{1,2,0:T(8,128)(2,1)} copy(bf16[6,360,384]{2,1,0:T(8,128)(2,1)} %param.10) | data formatting | bytes 3317760 | tf_op args[4]
  36.3 1.3 dynamic_slice.6.mine_ref
  37.6 1.8 dynamic-slice_bitcast_fusion.filter_ref
  39.4 38.2 %all-to-all-done = bf16[64,3,2,1152]{3,2,1,0:T(2,128)(2,1)} async-done(((bf16[64,3,2,1152]{3,2,1,0:T(2,128)(2,1)}), bf16[64,3,2,1152]{3,2,1,0:T(2,128)(2,1)}, u32[]{:S(2)}, u32[]{:S(2)}) %all-to-all-start) | async-done | bytes 884768 | tf_op jit(solution)/shard_map/all_to_all | solution.py:236
  77.5 6.2 %legendre.1 = bf16[192,2,1152]{2,1,0:T(2,128)(2,1)} custom-call(s32[6]{0:T(128)} %dynamic_slice.6.mine_ref, bf16[192,2,1152]{2,1,0:T(2,128)(2,1)} %bitcast.4.x_ref, bf16[6,360,384]{2,1,0:T(8,128)(2,1)} %bitcast.24, bf16[6,384,360]{2,1,0:T(8,128)(2,1)} %bitcast.17, f32[360,96]{1,0:T(8,128)} %dynamic-slice_bitcast_fusion.filter_ref), custom_call_target="tpu_custom_call" | custom-call | tf_op jit(solution)/shard_map/legendre/pallas_call | solution.py:141
  83.7 10.8 %all-to-all-start.1 = ((bf16[64,3,2,1152]{3,2,1,0:T(2,128)(2,1)}), bf16[64,3,2,1152]{3,2,1,0:T(2,128)(2,1)}, u32[]{:S(2)}, u32[]{:S(2)}) async-start(bf16[64,3,2,1152]{3,2,1,0:T(2,128)(2,1)} %bitcast.21), calls=%async_computation.1 | async-start | bytes 1769472 | tf_op jit(solution)/shard_map/all_to_all | solution.py:243
  94.5 2.8 %inverse_table.1.table_ref = bf16[768,720]{1,0:T(8,128)(2,1)} custom-call(s32[1,384]{1,0:T(1,128)} %reshape.24.orders_ref), custom_call_target="tpu_custom_call" | custom-call | tf_op jit(solution)/shard_map/inverse_table/pallas_call | solution.py:112
  97.3 2.1 %fusion.seen_ref = bf16[6,96,720]{2,1,0:T(8,128)(2,1)} fusion(bf16[6,384,720]{1,2,0:T(8,128)(2,1)S(1)} %copy-done, s32[96]{0:T(128)S(1)} %iota_add_fusion), kind=kOutput, calls=%fused_computation.1 | convolution fusion | flops 318956544 | bytes 4147584 | tf_op jit(solution)/shard_map/qc,tck->tqk/dot_general | solution.py:246
  99.4 39.7 %all-to-all-done.1 = bf16[64,3,2,1152]{3,2,1,0:T(2,128)(2,1)} async-done(((bf16[64,3,2,1152]{3,2,1,0:T(2,128)(2,1)}), bf16[64,3,2,1152]{3,2,1,0:T(2,128)(2,1)}, u32[]{:S(2)}, u32[]{:S(2)}) %all-to-all-start.1) | async-done | bytes 884768 | tf_op jit(solution)/shard_map/all_to_all | solution.py:243
  139.1 5.1 %synthesise.1 = (bf16[6,96,720]{2,1,0:T(8,128)(2,1)}, bf16[4,96,720]{2,1,0:T(8,128)(2,1)}, bf16[2,96,720]{2,1,0:T(8,128)(2,1)}) custom-call(bf16[768,720]{1,0:T(8,128)(2,1)} %inverse_table.1.table_ref, bf16[192,2,1152]{2,1,0:T(2,128)(2,1)} %bitcast.9.x_ref, bf16[6,96,720]{2,1,0:T(8,128)(2,1)} %bitcast.19), custom_call_target="tpu_custom_call" | custom-call | tf_op jit(solution)/shard_map/synthesise/pallas_call | solution.py:185
  144.2 3.1 %collective-permute-start.4 = (bf16[4,96,720]{2,1,0:T(8,128)(2,1)}, bf16[4,96,720]{2,1,0:T(8,128)(2,1)S(1)}, u32[]{:S(2)}, u32[]{:S(2)}) collective-permute-start(bf16[4,96,720]{2,1,0:T(8,128)(2,1)} %get-tuple-element.19), channel_id=1, source_target_pairs={{0,128},{64,192},{128,0},{192,64},{256,384},{320,448},{384,256},{4... | collective-permute-start | bytes 1658888 | tf_op jit(solution)/shard_map/ppermute | solution.py:254
  147.3 6.7 %collective-permute-start.3 = (bf16[4,96,720]{2,1,0:T(8,128)(2,1)}, bf16[4,96,720]{2,1,0:T(8,128)(2,1)S(1)}, u32[]{:S(2)}, u32[]{:S(2)}) collective-permute-start(bf16[4,96,720]{2,1,0:T(8,128)(2,1)} %get-tuple-element.19), channel_id=1, source_target_pairs={{0,64},{64,0},{128,192},{192,128},{256,320},{320,256},{384,448},{4... | collective-permute-start | bytes 1658888 | tf_op jit(solution)/shard_map/ppermute | solution.py:255
  154.0 2.6 %collective-permute-done.4.far_ref = bf16[4,96,720]{2,1,0:T(8,128)(2,1)S(1)} collective-permute-done((bf16[4,96,720]{2,1,0:T(8,128)(2,1)}, bf16[4,96,720]{2,1,0:T(8,128)(2,1)S(1)}, u32[]{:S(2)}, u32[]{:S(2)}) %collective-permute-start.4) | collective-permute-done | bytes 552992 | tf_op jit(solution)/shard_map/ppermute | solution.py:254
  156.6 0.8 copy-done.1
  157.4 7.3 %collective-permute-start.5 = (bf16[4,96,720]{2,1,0:T(8,128)(2,1)S(1)}, bf16[4,96,720]{2,1,0:T(8,128)(2,1)S(1)}, u32[]{:S(2)}, u32[]{:S(2)}) collective-permute-start(bf16[4,96,720]{2,1,0:T(8,128)(2,1)S(1)} %collective-permute-done.4.far_ref), channel_id=1, source_target_pairs={{0,64},{64,0},{128,192},{192,128},{256,320},{320,256},{384,448},{4... | collective-permute-start | bytes 1658888 | tf_op jit(solution)/shard_map/ppermute | solution.py:256
  164.7 3.1 %collective-permute-start.1 = (bf16[2,96,720]{2,1,0:T(8,128)(2,1)}, bf16[2,96,720]{2,1,0:T(8,128)(2,1)}, u32[]{:S(2)}, u32[]{:S(2)}) collective-permute-start(bf16[2,96,720]{2,1,0:T(8,128)(2,1)} %get-tuple-element.17), channel_id=1, source_target_pairs={{0,128},{64,192},{128,0},{192,64},{256,384},{320,448},{384,256},{4... | collective-permute-start | bytes 829448 | tf_op jit(solution)/shard_map/ppermute | solution.py:254
  167.9 2.2 %collective-permute-start = (bf16[2,96,720]{2,1,0:T(8,128)(2,1)}, bf16[2,96,720]{2,1,0:T(8,128)(2,1)}, u32[]{:S(2)}, u32[]{:S(2)}) collective-permute-start(bf16[2,96,720]{2,1,0:T(8,128)(2,1)} %get-tuple-element.17), channel_id=1, source_target_pairs={{0,64},{64,0},{128,192},{192,128},{256,320},{320,256},{384,448},{4... | collective-permute-start | bytes 829448 | tf_op jit(solution)/shard_map/ppermute | solution.py:255
  170.1 5.4 %collective-permute-done.1.far_ref = bf16[2,96,720]{2,1,0:T(8,128)(2,1)} collective-permute-done((bf16[2,96,720]{2,1,0:T(8,128)(2,1)}, bf16[2,96,720]{2,1,0:T(8,128)(2,1)}, u32[]{:S(2)}, u32[]{:S(2)}) %collective-permute-start.1) | collective-permute-done | bytes 276512 | tf_op jit(solution)/shard_map/ppermute | solution.py:254
  175.5 2.8 %collective-permute-start.2 = (bf16[2,96,720]{2,1,0:T(8,128)(2,1)}, bf16[2,96,720]{2,1,0:T(8,128)(2,1)}, u32[]{:S(2)}, u32[]{:S(2)}) collective-permute-start(bf16[2,96,720]{2,1,0:T(8,128)(2,1)} %collective-permute-done.1.far_ref), channel_id=1, source_target_pairs={{0,64},{64,0},{128,192},{192,128},{256,320},{320,256},{384,448},{4... | collective-permute-start | bytes 829448 | tf_op jit(solution)/shard_map/ppermute | solution.py:256
  178.3 0.0 collective-permute-done.3.near_ref
  178.3 0.0 copy-start.2
  178.3 0.0 collective-permute-done.5.far_near_ref
  178.3 0.8 copy-done.2
  179.1 0.8 copy-done.3
  180.0 4.3 %crps.2.rest_0_ = bf16[6,96,720]{2,1,0:T(8,128)(2,1)} custom-call(bf16[6,96,720]{2,1,0:T(8,128)(2,1)} %get-tuple-element.16.own_ref, bf16[4,96,720]{2,1,0:T(8,128)(2,1)} %copy-done.2, bf16[4,96,720]{2,1,0:T(8,128)(2,1)} %copy-done.1, bf16[4,96,720]{2,1,0:T(8,128)(2,1)} %copy-done.3, bf16[6,96,720]{2,1,0:T(8,128)(2,1)} %fusion.seen_ref), custom_call_target="tpu_custom_call" | custom-call | tf_op jit(solution)/shard_map/crps/pallas_call | solution.py:215
  184.2 0.0 collective-permute-done.near_ref
  184.2 0.0 collective-permute-done.2.far_near_ref
  184.2 2.5 %crps.3 = bf16[6,96,720]{2,1,0:T(8,128)(2,1)} custom-call(bf16[6,96,720]{2,1,0:T(8,128)(2,1)} %get-tuple-element.16.own_ref, bf16[2,96,720]{2,1,0:T(8,128)(2,1)} %collective-permute-done.near_ref, bf16[2,96,720]{2,1,0:T(8,128)(2,1)} %collective-permute-done.1.far_ref, ...), custom_call_target="tpu_custom_call", output_to_operand_aliasing={{}: (5, {})} | custom-call | tf_op jit(solution)/shard_map/crps/pallas_call | solution.py:215
  (4 shorter events, 0.0 us)
Async XLA Ops:
  0.6 96.7 %copy-start = (bf16[6,384,720]{1,2,0:T(8,128)(2,1)S(1)}, bf16[6,384,720]{1,2,0:T(8,128)(2,1)}, u32[]{:S(2)}) copy-start(bf16[6,384,720]{1,2,0:T(8,128)(2,1)} %param.7) | copy-start | bytes 9953284
  6.7 70.8 %all-to-all-start = ((bf16[64,3,2,1152]{3,2,1,0:T(2,128)(2,1)}), bf16[64,3,2,1152]{3,2,1,0:T(2,128)(2,1)}, u32[]{:S(2)}, u32[]{:S(2)}) async-start(bf16[64,3,2,1152]{3,2,1,0:T(2,128)(2,1)} %bitcast.20), calls=%async_computation | async-start | bytes 1769472 | tf_op jit(solution)/shard_map/all_to_all | solution.py:236
  83.7 55.4 %all-to-all-start.1 = ((bf16[64,3,2,1152]{3,2,1,0:T(2,128)(2,1)}), bf16[64,3,2,1152]{3,2,1,0:T(2,128)(2,1)}, u32[]{:S(2)}, u32[]{:S(2)}) async-start(bf16[64,3,2,1152]{3,2,1,0:T(2,128)(2,1)} %bitcast.21), calls=%async_computation.1 | async-start | bytes 1769472 | tf_op jit(solution)/shard_map/all_to_all | solution.py:243
  144.2 12.4 %collective-permute-start.4 = (bf16[4,96,720]{2,1,0:T(8,128)(2,1)}, bf16[4,96,720]{2,1,0:T(8,128)(2,1)S(1)}, u32[]{:S(2)}, u32[]{:S(2)}) collective-permute-start(bf16[4,96,720]{2,1,0:T(8,128)(2,1)} %get-tuple-element.19), channel_id=1, source_target_pairs={{0,128},{64,192},{128,0},{192,64},{256,384},{320,448},{384,256},{4... | collective-permute-start | bytes 1658888 | tf_op jit(solution)/shard_map/ppermute | solution.py:254
  147.3 31.0 %collective-permute-start.3 = (bf16[4,96,720]{2,1,0:T(8,128)(2,1)}, bf16[4,96,720]{2,1,0:T(8,128)(2,1)S(1)}, u32[]{:S(2)}, u32[]{:S(2)}) collective-permute-start(bf16[4,96,720]{2,1,0:T(8,128)(2,1)} %get-tuple-element.19), channel_id=1, source_target_pairs={{0,64},{64,0},{128,192},{192,128},{256,320},{320,256},{384,448},{4... | collective-permute-start | bytes 1658888 | tf_op jit(solution)/shard_map/ppermute | solution.py:255
  156.6 0.8 copy-start.1
  157.4 20.9 %collective-permute-start.5 = (bf16[4,96,720]{2,1,0:T(8,128)(2,1)S(1)}, bf16[4,96,720]{2,1,0:T(8,128)(2,1)S(1)}, u32[]{:S(2)}, u32[]{:S(2)}) collective-permute-start(bf16[4,96,720]{2,1,0:T(8,128)(2,1)S(1)} %collective-permute-done.4.far_ref), channel_id=1, source_target_pairs={{0,64},{64,0},{128,192},{192,128},{256,320},{320,256},{384,448},{4... | collective-permute-start | bytes 1658888 | tf_op jit(solution)/shard_map/ppermute | solution.py:256
  164.7 10.8 %collective-permute-start.1 = (bf16[2,96,720]{2,1,0:T(8,128)(2,1)}, bf16[2,96,720]{2,1,0:T(8,128)(2,1)}, u32[]{:S(2)}, u32[]{:S(2)}) collective-permute-start(bf16[2,96,720]{2,1,0:T(8,128)(2,1)} %get-tuple-element.17), channel_id=1, source_target_pairs={{0,128},{64,192},{128,0},{192,64},{256,384},{320,448},{384,256},{4... | collective-permute-start | bytes 829448 | tf_op jit(solution)/shard_map/ppermute | solution.py:254
  167.9 16.4 %collective-permute-start = (bf16[2,96,720]{2,1,0:T(8,128)(2,1)}, bf16[2,96,720]{2,1,0:T(8,128)(2,1)}, u32[]{:S(2)}, u32[]{:S(2)}) collective-permute-start(bf16[2,96,720]{2,1,0:T(8,128)(2,1)} %get-tuple-element.17), channel_id=1, source_target_pairs={{0,64},{64,0},{128,192},{192,128},{256,320},{320,256},{384,448},{4... | collective-permute-start | bytes 829448 | tf_op jit(solution)/shard_map/ppermute | solution.py:255
  175.5 8.7 %collective-permute-start.2 = (bf16[2,96,720]{2,1,0:T(8,128)(2,1)}, bf16[2,96,720]{2,1,0:T(8,128)(2,1)}, u32[]{:S(2)}, u32[]{:S(2)}) collective-permute-start(bf16[2,96,720]{2,1,0:T(8,128)(2,1)} %collective-permute-done.1.far_ref), channel_id=1, source_target_pairs={{0,64},{64,0},{128,192},{192,128},{256,320},{320,256},{384,448},{4... | collective-permute-start | bytes 829448 | tf_op jit(solution)/shard_map/ppermute | solution.py:256
  178.3 0.8 copy-start.2
  179.1 0.8 copy-start.3

commit v3 on v2

--- a/solution.py
+++ b/solution.py
@@ -8,11 +8,13 @@
 from jax.experimental.pallas import tpu as pltpu
 from jax.sharding import PartitionSpec as P
 
+
 ENS = 4
 BF = jnp.bfloat16
 F32 = jnp.float32
 smooth_sq = 0.25
 LANES = 128
+CHUNKS = 3
 GROUP = 2
 
 
@@ -37,11 +39,11 @@
 
 
 def fill_table(orders_ref, table_ref, bands, lon_count, degree_total, scale):
-    slots = orders_ref.shape[1]
+    slots = orders_ref.shape[0]
     mine = slots // bands
     shape = (bands, LANES)
     lane = lax.broadcasted_iota(jnp.int32, shape, 1).astype(F32)
-    every = orders_ref[...].astype(F32)
+    every = orders_ref[...].reshape(1, slots).astype(F32)
     first = mine * lax.broadcasted_iota(jnp.int32, (bands, slots), 0)
     place = lax.broadcasted_iota(jnp.int32, (bands, slots), 1)
     for s in range(mine):
@@ -91,7 +93,7 @@
 
 def analyse(orders, field, bands, degree_total):
     lat, chan, lon = field.shape
-    pieces = 2 * orders.shape[1] // bands
+    pieces = 2 * orders.shape[0] // bands
     return pl.pallas_call(
         functools.partial(analyse_kernel, bands=bands, degree_total=degree_total),
         out_shape=jax.ShapeDtypeStruct((bands * lat // 2, 2, pieces * chan), BF),
@@ -111,7 +113,7 @@
 def inverse_table(orders, bands, lon_count, degree_total):
     return pl.pallas_call(
         functools.partial(table_kernel, bands=bands, degree_total=degree_total),
-        out_shape=jax.ShapeDtypeStruct((2 * orders.shape[1], lon_count), BF),
+        out_shape=jax.ShapeDtypeStruct((2 * orders.shape[0], lon_count), BF),
         name="inverse_table",
     )(orders)
 
@@ -156,43 +158,57 @@
     )(mine, x, a, s, filters)
 
 
-def synth_kernel(table_ref, x_ref, field_ref, out_ref, low_ref, high_ref, rows, cols):
-    lat, chan, lon = field_ref.shape
-    pieces = x_ref.shape[2] // chan
-    bands = table_ref.shape[0] // pieces
+def synth_kernel(table_ref, x_ref, field_ref, *rest):
+    out_ref, part_ref, rows, cols = rest[-4:]
+    count, chan, _ = field_ref.shape
+    bands = x_ref.shape[0]
+    pieces = table_ref.shape[0] // bands
     tiles = rows.shape[0]
-    first = low_ref.shape[0]
     for q in range(tiles):
-        rows[q] = x_ref[:, :, q * LANES : (q + 1) * LANES].reshape(lat * bands, LANES).astype(F32)
-    for t in range(lat):
-        line = jnp.concatenate([rows[q, pl.ds(t, bands, lat), :] for q in range(tiles)], 1).astype(BF)
+        tile = x_ref[:, 0, :, q * LANES : (q + 1) * LANES]
+        rows[q] = tile.reshape(count * bands, LANES).astype(F32)
+    for t in range(count):
+        line = [rows[q, pl.ds(t, bands, count), :] for q in range(tiles)]
+        line = jnp.concatenate(line, 1).astype(BF)
         for j in range(pieces):
-            cols[j * bands : (j + 1) * bands, :] = line[:, j * chan : (j + 1) * chan]
-        total = lax.dot_general(
-            cols[...], table_ref[...], (((0,), (0,)), ((), ())), preferred_element_type=F32
-        )
-        done = (field_ref[t].astype(F32) + total).astype(BF)
+            piece = line[:, j * chan : (j + 1) * chan]
+            cols[j * bands : (j + 1) * bands, t * chan : (t + 1) * chan] = piece
+    total = lax.dot_general(
+        cols[...], table_ref[...], (((0,), (0,)), ((), ())), preferred_element_type=F32
+    )
+    for t in range(count):
+        done = (field_ref[t].astype(F32) + total[t * chan : (t + 1) * chan]).astype(BF)
         out_ref[t] = done
-        if t < first:
-            low_ref[t] = done
-        else:
-            high_ref[t - first] = done
-
-
-def synthesise(table, x, field, first):
-    lat, chan, lon = field.shape
-    tiles = x.shape[2] // LANES
+        part_ref[t] = done
+
+
+def synthesise(table, x, field, place, filled=None):
+    _, chan, lon = field.shape
+    bands, _, count, width = x.shape
+    tiles = width // LANES
+    block = pl.BlockSpec((count, chan, lon), lambda i: (place, 0, 0))
+    more = [] if filled is None else [filled]
     return pl.pallas_call(
         synth_kernel,
+        grid=(1,),
+        in_specs=[
+            pl.BlockSpec(table.shape, lambda i: (0, 0)),
+            pl.BlockSpec((bands, 1, count, width), lambda i: (0, place, 0, 0)),
+            block,
+        ]
+        + [pl.BlockSpec(memory_space=pl.ANY)] * len(more),
+        out_specs=[block, pl.BlockSpec((count, chan, lon), lambda i: (0, 0, 0))],
         out_shape=[
-            jax.ShapeDtypeStruct((n, chan, lon), BF) for n in (lat, first, lat - first)
+            jax.ShapeDtypeStruct(field.shape, BF),
+            jax.ShapeDtypeStruct((count, chan, lon), BF),
         ],
+        input_output_aliases={3: 0} if more else {},
         scratch_shapes=[
-            pltpu.VMEM((tiles, x.shape[0] * 2, LANES), F32),
-            pltpu.VMEM((table.shape[0], chan), BF),
+            pltpu.VMEM((tiles, count * bands, LANES), F32),
+            pltpu.VMEM((table.shape[0], count * chan), BF),
         ],
         name="synthesise",
-    )(table, x, field)
+    )(table, x, field, *more)
 
 
 def crps_kernel(own_ref, near_ref, far_ref, far_near_ref, seen_ref, *rest):
@@ -208,14 +224,14 @@
 
 
 def crps(own, near, far, far_near, seen, start, filled=None):
-    lat, chan, lon = near.shape
+    lat, chan, lon = far.shape
     part = pl.BlockSpec((1, chan, lon), lambda t: (t, 0, 0))
     whole = pl.BlockSpec((1, chan, lon), lambda t: (t + start, 0, 0))
     more = [] if filled is None else [filled]
     return pl.pallas_call(
         crps_kernel,
         grid=(lat,),
-        in_specs=[whole, part, part, part, whole] + [pl.BlockSpec(memory_space=pl.ANY)] * len(more),
+        in_specs=[whole, whole, part, part, whole] + [pl.BlockSpec(memory_space=pl.ANY)] * len(more),
         out_specs=whole,
         out_shape=jax.ShapeDtypeStruct(own.shape, BF),
         input_output_aliases={5: 0} if more else {},
@@ -231,8 +247,7 @@
     width = 2 * mine_count * chan
     packed = (bands, lat // 2, 2, width)
     flat = (bands * lat // 2, 2, width)
-    orders = slot_orders.reshape(1, bands * mine_count)
-    spectral = analyse(orders, field[0], bands, degrees).reshape(packed)
+    spectral = analyse(slot_orders, field[0], bands, degrees).reshape(packed)
     got = lax.all_to_all(spectral, "polar", split_axis=0, concat_axis=0, tiled=True)
     group = lax.axis_index("ens") // ENS
     mine = lax.dynamic_slice_in_dim(slot_orders, lax.axis_index("polar") * mine_count, mine_count)
@@ -241,20 +256,24 @@
     got, turned, filters = lax.optimization_barrier((got, turned, filters))
     out = legendre(mine, got.reshape(flat), jnp.swapaxes(analysis, 1, 2), turned, filters)
     back = lax.all_to_all(out.reshape(packed), "polar", split_axis=0, concat_axis=0, tiled=True)
-    inverse = inverse_table(orders, bands, lon, degrees)
+    inverse = inverse_table(slot_orders, bands, lon, degrees)
     pick = (group * chan + jnp.arange(chan)[:, None] == jnp.arange(target.shape[1])[None, :]).astype(BF)
     seen = jnp.einsum("qc,tck->tqk", pick, target, preferred_element_type=F32).astype(BF)
     back, inverse, seen = lax.optimization_barrier((back, inverse, seen))
-    first = 4
-    prediction, low, high = synthesise(inverse, back.reshape(flat), field[0], first)
     across = [(i, i ^ 2) for i in range(ens)]
     beside = [(i, i ^ 1) for i in range(ens)]
-    gradient = None
-    for start, own in ((0, low), (first, high)):
-        far = lax.ppermute(own, "ens", across)
-        near = lax.ppermute(own, "ens", beside)
+    count = 2
+    prediction = gradient = None
+    fars = []
+    for k in range(CHUNKS):
+        prediction, part = synthesise(
+            inverse, back, field[0], k, prediction
+        )
+        fars.append(lax.ppermute(part, "ens", across))
+    near = lax.ppermute(prediction, "ens", beside)
+    for k, far in enumerate(fars):
         far_near = lax.ppermute(far, "ens", beside)
-        gradient = crps(prediction, near, far, far_near, seen, start, gradient)
+        gradient = crps(prediction, near, far, far_near, seen, k * count, gradient)
     return prediction[None], gradient[None]
 
 

time: 188 us -> 189 us (level)
  Pallas kernels: 25.5 us -> 30.3 us
  local copies, waits for them, and re-layouts: 10.8 us -> 8.29 us
    pallas_call x3 -> x6, Pallas kernels: 11.9 us -> 16.5 us  [the longest x3 9.04 us: synthesise(): pl.pallas_call(synth_kernel, grid=(1,), in_specs=[pl.BlockSpec(table.shap...]
    unnamed x9 -> x7, local copies, waits for them, and re-layouts: 6.3 us -> 5.23 us
    ppermute x2 -> x3, starting transfers between devices: 10.1 us -> 9.25 us  [body(): far_near = lax.ppermute(far, 'ens', beside)]
  transfers between devices with their start and end apart: 8 -> 9, of which waited for: 4 -> 5; matrix products, arithmetic and copies ran while one was open for 5% -> 5% of each run, Pallas kernels for 4% -> 4%
where the time goes in v3:
time: 189 us; the launch traced here: 188 us
  waiting for transfers between devices  85.6 us (45%)
  starting transfers between devices  60.7 us (32%)
  Pallas kernels  30.3 us (16%)
  local copies, waits for them, and re-layouts  8.29 us (4%)
  matrix products  2.1 us (1%)
    all_to_all x1, waiting for transfers between devices, body(): lax.all_to_all(out.reshape(packed), 'polar', split_axis=0, concat_axis=0,...  39.7 us
    all_to_all x1, waiting for transfers between devices, body(): lax.all_to_all(spectral, 'polar', split_axis=0, concat_axis=0, tiled=True)  38.1 us
    all_to_all x1, starting transfers between devices, body(): lax.all_to_all(spectral, 'polar', split_axis=0, concat_axis=0, tiled=True)  25.8 us
    all_to_all x1, starting transfers between devices, body(): lax.all_to_all(out.reshape(packed), 'polar', split_axis=0, concat_axis=0,...  10.8 us
    ppermute x3, starting transfers between devices, body(): far_near = lax.ppermute(far, 'ens', beside)  9.25 us
    pallas_call x3, Pallas kernels, synthesise(): pl.pallas_call(synth_kernel, grid=(1,), in_specs=[pl.BlockSpec(table.shap...  9.04 us
    ppermute x3, starting transfers between devices, body(): fars.append(lax.ppermute(part, 'ens', across))  8.4 us
    ppermute x3, waiting for transfers between devices, body(): fars.append(lax.ppermute(part, 'ens', across))  7.75 us
  transfers between devices with their start and end apart: 9, of which 5 were waited for; matrix products, arithmetic and copies ran while one was open for 5% of the time, Pallas kernels for 4%

profile of v3, /device:TPU:1, one launch (start us, length us, event | category | flops | bytes accessed | tf_op | source)
XLA Modules:
  0.0 187.7 jit_solution(9703006870003524316)
XLA Ops:
  0.6 0.0 copy-start
  0.6 4.8 %analyse.1 = bf16[192,2,1152]{2,1,0:T(2,128)(2,1)} custom-call(s32[384]{0:T(512)} %orders_ref.3, bf16[6,96,720]{2,1,0:T(8,128)(2,1)} %bitcast.17), custom_call_target="tpu_custom_call" | custom-call | tf_op jit(solution)/shard_map/analyse/pallas_call | solution.py:97
  5.4 25.8 %all-to-all-start = ((bf16[64,3,2,1152]{3,2,1,0:T(2,128)(2,1)}), bf16[64,3,2,1152]{3,2,1,0:T(2,128)(2,1)}, u32[]{:S(2)}, u32[]{:S(2)}) async-start(bf16[64,3,2,1152]{3,2,1,0:T(2,128)(2,1)} %bitcast.23), calls=%async_computation | async-start | bytes 1769472 | tf_op jit(solution)/shard_map/all_to_all | solution.py:251
  31.3 3.8 %copy.12 = bf16[6,360,384]{1,2,0:T(8,128)(2,1)} copy(bf16[6,360,384]{2,1,0:T(8,128)(2,1)} %param.10) | data formatting | bytes 3317760 | tf_op args[4]
  35.1 1.3 dynamic_slice.6.mine_ref
  36.3 1.8 dynamic-slice_bitcast_fusion.filter_ref
  38.1 38.1 %all-to-all-done = bf16[64,3,2,1152]{3,2,1,0:T(2,128)(2,1)} async-done(((bf16[64,3,2,1152]{3,2,1,0:T(2,128)(2,1)}), bf16[64,3,2,1152]{3,2,1,0:T(2,128)(2,1)}, u32[]{:S(2)}, u32[]{:S(2)}) %all-to-all-start) | async-done | bytes 884768 | tf_op jit(solution)/shard_map/all_to_all | solution.py:251
  76.2 6.2 %legendre.1 = bf16[192,2,1152]{2,1,0:T(2,128)(2,1)} custom-call(s32[6]{0:T(128)} %dynamic_slice.6.mine_ref, bf16[192,2,1152]{2,1,0:T(2,128)(2,1)} %bitcast.4.x_ref, bf16[6,360,384]{2,1,0:T(8,128)(2,1)} %bitcast.25, bf16[6,384,360]{2,1,0:T(8,128)(2,1)} %bitcast.22, f32[360,96]{1,0:T(8,128)} %dynamic-slice_bitcast_fusion.filter_ref), custom_call_target="tpu_custom_call" | custom-call | tf_op jit(solution)/shard_map/legendre/pallas_call | solution.py:143
  82.4 10.8 %all-to-all-start.1 = ((bf16[64,3,2,1152]{3,2,1,0:T(2,128)(2,1)}), bf16[64,3,2,1152]{3,2,1,0:T(2,128)(2,1)}, u32[]{:S(2)}, u32[]{:S(2)}) async-start(bf16[64,3,2,1152]{3,2,1,0:T(2,128)(2,1)} %bitcast.24), calls=%async_computation.1 | async-start | bytes 1769472 | tf_op jit(solution)/shard_map/all_to_all | solution.py:258
  93.2 2.8 %inverse_table.1.table_ref = bf16[768,720]{1,0:T(8,128)(2,1)} custom-call(s32[384]{0:T(512)} %orders_ref.3), custom_call_target="tpu_custom_call" | custom-call | tf_op jit(solution)/shard_map/inverse_table/pallas_call | solution.py:114
  96.0 2.1 %fusion.seen_ref = bf16[6,96,720]{2,1,0:T(8,128)(2,1)} fusion(bf16[6,384,720]{1,2,0:T(8,128)(2,1)S(1)} %copy-done, s32[96]{0:T(128)S(1)} %iota_add_fusion), kind=kOutput, calls=%fused_computation.1 | convolution fusion | flops 318956544 | bytes 4147584 | tf_op jit(solution)/shard_map/qc,tck->tqk/dot_general | solution.py:261
  98.1 39.7 %all-to-all-done.1.x_ref = bf16[64,3,2,1152]{3,2,1,0:T(2,128)(2,1)} async-done(((bf16[64,3,2,1152]{3,2,1,0:T(2,128)(2,1)}), bf16[64,3,2,1152]{3,2,1,0:T(2,128)(2,1)}, u32[]{:S(2)}, u32[]{:S(2)}) %all-to-all-start.1) | async-done | bytes 884768 | tf_op jit(solution)/shard_map/all_to_all | solution.py:258
  137.8 3.0 %synthesise.3 = (bf16[6,96,720]{2,1,0:T(8,128)(2,1)}, bf16[2,96,720]{2,1,0:T(8,128)(2,1)}) custom-call(bf16[768,720]{1,0:T(8,128)(2,1)} %inverse_table.1.table_ref, bf16[64,3,2,1152]{3,2,1,0:T(2,128)(2,1)} %all-to-all-done.1.x_ref, bf16[6,96,720]{2,1,0:T(8,128)(2,1)} %bitcast.18), custom_call_target="tpu_custom_call" | custom-call | tf_op jit(solution)/shard_map/synthesise/pallas_call | solution.py:191
  140.8 3.0 %synthesise.4 = (bf16[6,96,720]{2,1,0:T(8,128)(2,1)}, bf16[2,96,720]{2,1,0:T(8,128)(2,1)}) custom-call(bf16[768,720]{1,0:T(8,128)(2,1)} %inverse_table.1.table_ref, bf16[64,3,2,1152]{3,2,1,0:T(2,128)(2,1)} %all-to-all-done.1.x_ref, bf16[6,96,720]{2,1,0:T(8,128)(2,1)} %bitcast.19, ...), custom_call_target="tpu_custom_call", output_to_operand_aliasing={{0}: (3, {})} | custom-call | tf_op jit(solution)/shard_map/synthesise/pallas_call | solution.py:191
  143.8 3.0 %synthesise.5 = (bf16[6,96,720]{2,1,0:T(8,128)(2,1)}, bf16[2,96,720]{2,1,0:T(8,128)(2,1)}) custom-call(bf16[768,720]{1,0:T(8,128)(2,1)} %inverse_table.1.table_ref, bf16[64,3,2,1152]{3,2,1,0:T(2,128)(2,1)} %all-to-all-done.1.x_ref, bf16[6,96,720]{2,1,0:T(8,128)(2,1)} %bitcast.20, ...), custom_call_target="tpu_custom_call", output_to_operand_aliasing={{0}: (3, {})} | custom-call | tf_op jit(solution)/shard_map/synthesise/pallas_call | solution.py:191
  146.8 6.4 %collective-permute-start = (bf16[6,96,720]{2,1,0:T(8,128)(2,1)}, bf16[6,96,720]{2,1,0:T(8,128)(2,1)}, u32[]{:S(2)}, u32[]{:S(2)}) collective-permute-start(bf16[6,96,720]{2,1,0:T(8,128)(2,1)} %get-tuple-element.21.own_ref), channel_id=1, source_target_pairs={{0,64},{64,0},{128,192},{192,128},{256,320},{320,256},{384,448},{4... | collective-permute-start | bytes 2488328 | tf_op jit(solution)/shard_map/ppermute | solution.py:273
  153.3 3.1 %collective-permute-start.5 = (bf16[2,96,720]{2,1,0:T(8,128)(2,1)}, bf16[2,96,720]{2,1,0:T(8,128)(2,1)S(1)}, u32[]{:S(2)}, u32[]{:S(2)}) collective-permute-start(bf16[2,96,720]{2,1,0:T(8,128)(2,1)} %get-tuple-element.25), channel_id=1, source_target_pairs={{0,128},{64,192},{128,0},{192,64},{256,384},{320,448},{384,256},{4... | collective-permute-start | bytes 829448 | tf_op jit(solution)/shard_map/ppermute | solution.py:272
  156.4 2.2 %collective-permute-start.3 = (bf16[2,96,720]{2,1,0:T(8,128)(2,1)}, bf16[2,96,720]{2,1,0:T(8,128)(2,1)}, u32[]{:S(2)}, u32[]{:S(2)}) collective-permute-start(bf16[2,96,720]{2,1,0:T(8,128)(2,1)} %get-tuple-element.24), channel_id=1, source_target_pairs={{0,128},{64,192},{128,0},{192,64},{256,384},{320,448},{384,256},{4... | collective-permute-start | bytes 829448 | tf_op jit(solution)/shard_map/ppermute | solution.py:272
  158.6 3.1 %collective-permute-start.1 = (bf16[2,96,720]{2,1,0:T(8,128)(2,1)}, bf16[2,96,720]{2,1,0:T(8,128)(2,1)}, u32[]{:S(2)}, u32[]{:S(2)}) collective-permute-start(bf16[2,96,720]{2,1,0:T(8,128)(2,1)} %get-tuple-element.22), channel_id=1, source_target_pairs={{0,128},{64,192},{128,0},{192,64},{256,384},{320,448},{384,256},{4... | collective-permute-start | bytes 829448 | tf_op jit(solution)/shard_map/ppermute | solution.py:272
  161.7 2.2 %collective-permute-done.5.far_ref = bf16[2,96,720]{2,1,0:T(8,128)(2,1)S(1)} collective-permute-done((bf16[2,96,720]{2,1,0:T(8,128)(2,1)}, bf16[2,96,720]{2,1,0:T(8,128)(2,1)S(1)}, u32[]{:S(2)}, u32[]{:S(2)}) %collective-permute-start.5) | collective-permute-done | bytes 276512 | tf_op jit(solution)/shard_map/ppermute | solution.py:272
  163.9 0.7 copy-done.1
  164.7 3.2 %collective-permute-start.6 = (bf16[2,96,720]{2,1,0:T(8,128)(2,1)S(1)}, bf16[2,96,720]{2,1,0:T(8,128)(2,1)S(1)}, u32[]{:S(2)}, u32[]{:S(2)}) collective-permute-start(bf16[2,96,720]{2,1,0:T(8,128)(2,1)S(1)} %collective-permute-done.5.far_ref), channel_id=1, source_target_pairs={{0,64},{64,0},{128,192},{192,128},{256,320},{320,256},{384,448},{4... | collective-permute-start | bytes 829448 | tf_op jit(solution)/shard_map/ppermute | solution.py:275
  167.9 2.4 %collective-permute-done.3.far_ref = bf16[2,96,720]{2,1,0:T(8,128)(2,1)} collective-permute-done((bf16[2,96,720]{2,1,0:T(8,128)(2,1)}, bf16[2,96,720]{2,1,0:T(8,128)(2,1)}, u32[]{:S(2)}, u32[]{:S(2)}) %collective-permute-start.3) | collective-permute-done | bytes 276512 | tf_op jit(solution)/shard_map/ppermute | solution.py:272
  170.4 3.2 %collective-permute-start.4 = (bf16[2,96,720]{2,1,0:T(8,128)(2,1)}, bf16[2,96,720]{2,1,0:T(8,128)(2,1)}, u32[]{:S(2)}, u32[]{:S(2)}) collective-permute-start(bf16[2,96,720]{2,1,0:T(8,128)(2,1)} %collective-permute-done.3.far_ref), channel_id=1, source_target_pairs={{0,64},{64,0},{128,192},{192,128},{256,320},{320,256},{384,448},{4... | collective-permute-start | bytes 829448 | tf_op jit(solution)/shard_map/ppermute | solution.py:275
  173.6 3.1 %collective-permute-done.1.far_ref = bf16[2,96,720]{2,1,0:T(8,128)(2,1)} collective-permute-done((bf16[2,96,720]{2,1,0:T(8,128)(2,1)}, bf16[2,96,720]{2,1,0:T(8,128)(2,1)}, u32[]{:S(2)}, u32[]{:S(2)}) %collective-permute-start.1) | collective-permute-done | bytes 276512 | tf_op jit(solution)/shard_map/ppermute | solution.py:272
  176.7 2.8 %collective-permute-start.2 = (bf16[2,96,720]{2,1,0:T(8,128)(2,1)}, bf16[2,96,720]{2,1,0:T(8,128)(2,1)}, u32[]{:S(2)}, u32[]{:S(2)}) collective-permute-start(bf16[2,96,720]{2,1,0:T(8,128)(2,1)} %collective-permute-done.1.far_ref), channel_id=1, source_target_pairs={{0,64},{64,0},{128,192},{192,128},{256,320},{320,256},{384,448},{4... | collective-permute-start | bytes 829448 | tf_op jit(solution)/shard_map/ppermute | solution.py:275
  179.5 0.0 collective-permute-done.6.far_near_ref
  179.5 0.7 copy-done.2
  180.2 0.0 collective-permute-done.near_ref
  180.2 2.5 %crps.3.rest_0_ = bf16[6,96,720]{2,1,0:T(8,128)(2,1)} custom-call(bf16[6,96,720]{2,1,0:T(8,128)(2,1)} %get-tuple-element.21.own_ref, bf16[6,96,720]{2,1,0:T(8,128)(2,1)} %collective-permute-done.near_ref, bf16[2,96,720]{2,1,0:T(8,128)(2,1)} %copy-done.1, bf16[2,96,720]{2,1,0:T(8,128)(2,1)} %copy-done.2, bf16[6,96,720]{2,1,0:T(8,128)(2,1)} %fusion.seen_ref), custom_call_target="tpu_custom_call" | custom-call | tf_op jit(solution)/shard_map/crps/pallas_call | solution.py:231
  182.7 2.5 %crps.4.rest_0_ = bf16[6,96,720]{2,1,0:T(8,128)(2,1)} custom-call(bf16[6,96,720]{2,1,0:T(8,128)(2,1)} %get-tuple-element.21.own_ref, bf16[6,96,720]{2,1,0:T(8,128)(2,1)} %collective-permute-done.near_ref, bf16[2,96,720]{2,1,0:T(8,128)(2,1)} %collective-permute-done.3.far_ref, ...), custom_call_target="tpu_custom_call", output_to_operand_aliasing={{}: (5, {})} | custom-call | tf_op jit(solution)/shard_map/crps/pallas_call | solution.py:231
  185.2 2.5 %crps.5 = bf16[6,96,720]{2,1,0:T(8,128)(2,1)} custom-call(bf16[6,96,720]{2,1,0:T(8,128)(2,1)} %get-tuple-element.21.own_ref, bf16[6,96,720]{2,1,0:T(8,128)(2,1)} %collective-permute-done.near_ref, bf16[2,96,720]{2,1,0:T(8,128)(2,1)} %collective-permute-done.1.far_ref, ...), custom_call_target="tpu_custom_call", output_to_operand_aliasing={{}: (5, {})} | custom-call | tf_op jit(solution)/shard_map/crps/pallas_call | solution.py:231
  (6 shorter events, 0.0 us)
Async XLA Ops:
  0.6 95.4 %copy-start = (bf16[6,384,720]{1,2,0:T(8,128)(2,1)S(1)}, bf16[6,384,720]{1,2,0:T(8,128)(2,1)}, u32[]{:S(2)}) copy-start(bf16[6,384,720]{1,2,0:T(8,128)(2,1)} %param.7) | copy-start | bytes 9953284
  5.4 70.8 %all-to-all-start = ((bf16[64,3,2,1152]{3,2,1,0:T(2,128)(2,1)}), bf16[64,3,2,1152]{3,2,1,0:T(2,128)(2,1)}, u32[]{:S(2)}, u32[]{:S(2)}) async-start(bf16[64,3,2,1152]{3,2,1,0:T(2,128)(2,1)} %bitcast.23), calls=%async_computation | async-start | bytes 1769472 | tf_op jit(solution)/shard_map/all_to_all | solution.py:251
  82.4 55.4 %all-to-all-start.1 = ((bf16[64,3,2,1152]{3,2,1,0:T(2,128)(2,1)}), bf16[64,3,2,1152]{3,2,1,0:T(2,128)(2,1)}, u32[]{:S(2)}, u32[]{:S(2)}) async-start(bf16[64,3,2,1152]{3,2,1,0:T(2,128)(2,1)} %bitcast.24), calls=%async_computation.1 | async-start | bytes 1769472 | tf_op jit(solution)/shard_map/all_to_all | solution.py:258
  146.8 33.4 %collective-permute-start = (bf16[6,96,720]{2,1,0:T(8,128)(2,1)}, bf16[6,96,720]{2,1,0:T(8,128)(2,1)}, u32[]{:S(2)}, u32[]{:S(2)}) collective-permute-start(bf16[6,96,720]{2,1,0:T(8,128)(2,1)} %get-tuple-element.21.own_ref), channel_id=1, source_target_pairs={{0,64},{64,0},{128,192},{192,128},{256,320},{320,256},{384,448},{4... | collective-permute-start | bytes 2488328 | tf_op jit(solution)/shard_map/ppermute | solution.py:273
  153.3 10.7 %collective-permute-start.5 = (bf16[2,96,720]{2,1,0:T(8,128)(2,1)}, bf16[2,96,720]{2,1,0:T(8,128)(2,1)S(1)}, u32[]{:S(2)}, u32[]{:S(2)}) collective-permute-start(bf16[2,96,720]{2,1,0:T(8,128)(2,1)} %get-tuple-element.25), channel_id=1, source_target_pairs={{0,128},{64,192},{128,0},{192,64},{256,384},{320,448},{384,256},{4... | collective-permute-start | bytes 829448 | tf_op jit(solution)/shard_map/ppermute | solution.py:272
  156.4 14.0 %collective-permute-start.3 = (bf16[2,96,720]{2,1,0:T(8,128)(2,1)}, bf16[2,96,720]{2,1,0:T(8,128)(2,1)}, u32[]{:S(2)}, u32[]{:S(2)}) collective-permute-start(bf16[2,96,720]{2,1,0:T(8,128)(2,1)} %get-tuple-element.24), channel_id=1, source_target_pairs={{0,128},{64,192},{128,0},{192,64},{256,384},{320,448},{384,256},{4... | collective-permute-start | bytes 829448 | tf_op jit(solution)/shard_map/ppermute | solution.py:272
  158.6 18.1 %collective-permute-start.1 = (bf16[2,96,720]{2,1,0:T(8,128)(2,1)}, bf16[2,96,720]{2,1,0:T(8,128)(2,1)}, u32[]{:S(2)}, u32[]{:S(2)}) collective-permute-start(bf16[2,96,720]{2,1,0:T(8,128)(2,1)} %get-tuple-element.22), channel_id=1, source_target_pairs={{0,128},{64,192},{128,0},{192,64},{256,384},{320,448},{384,256},{4... | collective-permute-start | bytes 829448 | tf_op jit(solution)/shard_map/ppermute | solution.py:272
  163.9 0.7 copy-start.1
  164.7 14.8 %collective-permute-start.6 = (bf16[2,96,720]{2,1,0:T(8,128)(2,1)S(1)}, bf16[2,96,720]{2,1,0:T(8,128)(2,1)S(1)}, u32[]{:S(2)}, u32[]{:S(2)}) collective-permute-start(bf16[2,96,720]{2,1,0:T(8,128)(2,1)S(1)} %collective-permute-done.5.far_ref), channel_id=1, source_target_pairs={{0,64},{64,0},{128,192},{192,128},{256,320},{320,256},{384,448},{4... | collective-permute-start | bytes 829448 | tf_op jit(solution)/shard_map/ppermute | solution.py:275
  170.4 12.3 %collective-permute-start.4 = (bf16[2,96,720]{2,1,0:T(8,128)(2,1)}, bf16[2,96,720]{2,1,0:T(8,128)(2,1)}, u32[]{:S(2)}, u32[]{:S(2)}) collective-permute-start(bf16[2,96,720]{2,1,0:T(8,128)(2,1)} %collective-permute-done.3.far_ref), channel_id=1, source_target_pairs={{0,64},{64,0},{128,192},{192,128},{256,320},{320,256},{384,448},{4... | collective-permute-start | bytes 829448 | tf_op jit(solution)/shard_map/ppermute | solution.py:275
  176.7 8.5 %collective-permute-start.2 = (bf16[2,96,720]{2,1,0:T(8,128)(2,1)}, bf16[2,96,720]{2,1,0:T(8,128)(2,1)}, u32[]{:S(2)}, u32[]{:S(2)}) collective-permute-start(bf16[2,96,720]{2,1,0:T(8,128)(2,1)} %collective-permute-done.1.far_ref), channel_id=1, source_target_pairs={{0,64},{64,0},{128,192},{192,128},{256,320},{320,256},{384,448},{4... | collective-permute-start | bytes 829448 | tf_op jit(solution)/shard_map/ppermute | solution.py:275
  179.5 0.7 copy-start.2

commit v4 on v3

v4 whole, which is shorter than its diff:
```python
import functools
import math

import jax
import jax.numpy as jnp
from jax import lax
from jax.experimental import pallas as pl
from jax.experimental.pallas import tpu as pltpu
from jax.sharding import PartitionSpec as P


ENS = 4
BF = jnp.bfloat16
F32 = jnp.float32
smooth_sq = 0.25
LANES = 128
CHUNKS = 3
VMEM = pl.BlockSpec(memory_space=pltpu.VMEM)
LIMIT = pltpu.CompilerParams(vmem_limit_bytes=20 << 20)


def on_chip(*arrays):
    return [pltpu.with_memory_space_constraint(a, pltpu.VMEM) for a in arrays]


def off_chip(*arrays):
    return [pltpu.with_memory_space_constraint(a, pltpu.HBM) for a in arrays]


GROUP = 2


def turn_sine(turns):
    w = turns * (2.0 * math.pi)
    w2 = w * w
    poly = -2.5052108e-8 + w2 * 1.6059044e-10
    for coef in (2.7557319e-6, -1.9841270e-4, 8.3333333e-3, -1.6666667e-1, 1.0):
        poly = poly * w2 + coef
    return poly * w


def cosine_sine(orders, points, lon_count):
    product = orders * points
    phase = product - jnp.floor(product * (1.0 / lon_count)) * lon_count
    turns = phase * (1.0 / lon_count)
    cosine = turn_sine(jnp.abs(turns - 0.5) - 0.25)
    shifted = turns + 0.75
    shifted = jnp.where(shifted >= 1.0, shifted - 1.0, shifted)
    sine = turn_sine(jnp.abs(shifted - 0.5) - 0.25)
    return cosine, sine


def fill_table(orders_ref, table_ref, bands, lon_count, degree_total, scale):
    slots = orders_ref.shape[0]
    mine = slots // bands
    shape = (bands, LANES)
    lane = lax.broadcasted_iota(jnp.int32, shape, 1).astype(F32)
    every = orders_ref[...].reshape(1, slots).astype(F32)
    first = mine * lax.broadcasted_iota(jnp.int32, (bands, slots), 0)
    place = lax.broadcasted_iota(jnp.int32, (bands, slots), 1)
    for s in range(mine):
        order = jnp.sum(jnp.where(place == first + s, every, 0.0), 1, keepdims=True)
        order = jnp.broadcast_to(order, shape)
        gain = jnp.where(order < degree_total, scale, 0.0)
        cosine, sine = cosine_sine(order, lane, lon_count)
        cosine, sine = cosine * gain, sine * gain
        turn_c, turn_s = cosine_sine(order, float(LANES), lon_count)
        low = 2 * s * bands
        for start in range(0, lon_count, LANES):
            width = min(LANES, lon_count - start)
            span = slice(start, start + width)
            table_ref[low : low + bands, span] = cosine[:, :width].astype(BF)
            table_ref[low + bands : low + 2 * bands, span] = (-sine[:, :width]).astype(BF)
            cosine, sine = cosine * turn_c - sine * turn_s, sine * turn_c + cosine * turn_s


def send(source, sink, sems, part, width):
    span = pl.ds(part * width, width)
    return pltpu.make_async_copy(source.at[:, :, span], sink.at[:, :, span], sems.at[part])


def analyse_kernel(orders_ref, source_ref, sink_ref, field_ref, out_ref, table, rows, sem, sent, *, bands, degree_total):
    lat, chan, lon = field_ref.shape
    pieces = table.shape[0] // bands
    copy = pltpu.make_async_copy(source_ref, field_ref, sem)
    copy.start()
    fill_table(orders_ref, table, bands, lon, degree_total, 1.0 / math.sqrt(lon))
    copy.wait()
    group = GROUP
    for t0 in range(0, lat, group):
        got = lax.dot_general(
            table[...],
            field_ref[t0 : t0 + group].reshape(group * chan, lon),
            (((1,), (1,)), ((), ())),
            preferred_element_type=F32,
        )
        for u in range(group):
            for start in range(0, pieces, 4):
                line = jnp.concatenate(
                    [
                        got[j * bands : (j + 1) * bands, u * chan : (u + 1) * chan]
                        for j in range(start, start + 4)
                    ],
                    1,
                )
                for q in range(4 * chan // LANES):
                    tile = start * chan // LANES + q
                    rows[tile, pl.ds(t0 + u, bands, lat), :] = line[:, q * LANES : (q + 1) * LANES]
    for q in range(rows.shape[0]):
        packed = rows[q].astype(BF).reshape(out_ref.shape[0], 2, LANES)
        out_ref[:, :, q * LANES : (q + 1) * LANES] = packed
        if q % 3 == 2:
            send(out_ref, sink_ref, sent, q // 3, 3 * LANES).start()
    for g in range(3):
        send(out_ref, sink_ref, sent, g, 3 * LANES).wait()


def analyse(orders, field, bands, degree_total):
    lat, chan, lon = field.shape
    pieces = 2 * orders.shape[0] // bands
    return pl.pallas_call(
        functools.partial(analyse_kernel, bands=bands, degree_total=degree_total),
        in_specs=[VMEM, pl.BlockSpec(memory_space=pl.ANY)],
        out_specs=pl.BlockSpec(memory_space=pl.ANY),
        out_shape=pltpu.HBM((bands * lat // 2, 2, pieces * chan), BF),
        scratch_shapes=[
            pltpu.VMEM(field.shape, BF),
            pltpu.VMEM((bands * lat // 2, 2, pieces * chan), BF),
            pltpu.VMEM((pieces * bands, lon), BF),
            pltpu.VMEM((pieces * chan // LANES, bands * lat, LANES), F32),
            pltpu.SemaphoreType.DMA,
            pltpu.SemaphoreType.DMA((3,)),
        ],
        compiler_params=LIMIT,
        name="analyse",
    )(orders, *off_chip(field))


def tables_kernel(group_ref, a_ref, s_ref, filter_ref, a_out, s_out, filter_out, sem):
    chan = filter_out.shape[1]
    copy = pltpu.make_async_copy(a_ref, a_out, sem)
    copy.start()
    for i in range(s_ref.shape[0]):
        s_out[i] = s_ref[i].astype(F32).T.astype(BF)
    group = group_ref[0]
    kept = filter_ref[:, :chan]
    for g in range(1, filter_ref.shape[1] // chan):
        kept = jnp.where(group == g, filter_ref[:, g * chan : (g + 1) * chan], kept)
    filter_out[...] = kept
    copy.wait()


def tables(group, a, s, filters, chan):
    slots, degrees, lat_all = a.shape
    return pl.pallas_call(
        tables_kernel,
        in_specs=[
            pl.BlockSpec(memory_space=pltpu.SMEM),
            pl.BlockSpec(memory_space=pl.ANY),
            VMEM,
            VMEM,
        ],
        out_specs=[VMEM] * 3,
        out_shape=[
            pltpu.VMEM(a.shape, BF),
            pltpu.HBM((slots, lat_all, degrees), BF),
            pltpu.VMEM((degrees, chan), F32),
        ],
        scratch_shapes=[pltpu.SemaphoreType.DMA],
        compiler_params=LIMIT,
        name="tables",
    )(group, *off_chip(a, s, filters))


def scene_kernel(
    group_ref, orders_ref, target_ref, source_ref, table_out, seen_out, field_out, sem, *, bands, degree_total
):
    lat, chan, lon = field_out.shape
    copy = pltpu.make_async_copy(source_ref, field_out, sem)
    copy.start()
    fill_table(orders_ref, table_out, bands, lon, degree_total, 1.0 / math.sqrt(degree_total))
    shape = (chan, target_ref.shape[2])
    place = lax.broadcasted_iota(jnp.int32, shape, 1) - group_ref[0] * chan
    pick = jnp.where(place == lax.broadcasted_iota(jnp.int32, shape, 0), 1.0, 0.0).astype(BF)
    for t in range(lat):
        seen = lax.dot_general(
            pick, target_ref[t], (((1,), (1,)), ((), ())), preferred_element_type=F32
        )
        seen_out[t] = seen.astype(BF)
    copy.wait()


def scene(group, orders, target, field, bands, degree_total):
    _, _, lon = field.shape
    return pl.pallas_call(
        functools.partial(scene_kernel, bands=bands, degree_total=degree_total),
        in_specs=[
            pl.BlockSpec(memory_space=pltpu.SMEM),
            VMEM,
            VMEM,
            pl.BlockSpec(memory_space=pl.ANY),
        ],
        out_specs=[VMEM] * 3,
        out_shape=[
            pltpu.VMEM((2 * orders.shape[0], lon), BF),
            pltpu.HBM(field.shape, BF),
            pltpu.VMEM(field.shape, BF),
        ],
        scratch_shapes=[pltpu.SemaphoreType.DMA],
        compiler_params=LIMIT,
        name="scene",
    )(group, orders, *off_chip(target, field))


def legendre_kernel(
    mine_ref, x_ref, a_ref, source_ref, filter_ref, sink_ref, s_ref, out_ref, come, sent
):
    slots, _, lat_all = a_ref.shape
    copies = [
        pltpu.make_async_copy(source_ref.at[i], s_ref.at[i], come.at[i]) for i in range(slots)
    ]
    for copy in copies:
        copy.start()
    chan = filter_ref.shape[1]
    degree = lax.broadcasted_iota(jnp.int32, filter_ref.shape, 0)
    for g in range(slots // 2):
        span = slice(g * 4 * chan, (g + 1) * 4 * chan)
        both = x_ref[:, :, span].reshape(lat_all, 4 * chan)
        outs = []
        for h in range(2):
            gain = jnp.where(degree >= mine_ref[2 * g + h], filter_ref[...], 0.0)
            gain = jnp.concatenate([gain, gain], 1)
            x = both[:, 2 * chan * h : 2 * chan * (h + 1)]
            coeffs = jnp.dot(a_ref[2 * g + h], x, preferred_element_type=F32)
            scaled = (coeffs * gain).astype(BF)
            copies[2 * g + h].wait()
            outs.append(jnp.dot(s_ref[2 * g + h], scaled, preferred_element_type=F32))
        out_ref[:, :, span] = jnp.concatenate(outs, 1).astype(BF).reshape(lat_all // 2, 2, 4 * chan)
        send(out_ref, sink_ref, sent, g, 4 * chan).start()
    for g in range(slots // 2):
        send(out_ref, sink_ref, sent, g, 4 * chan).wait()


def legendre(mine, x, a, s, filters):
    return pl.pallas_call(
        legendre_kernel,
        in_specs=[
            pl.BlockSpec(memory_space=pltpu.SMEM),
            VMEM,
            VMEM,
            pl.BlockSpec(memory_space=pl.ANY),
            VMEM,
        ],
        out_specs=pl.BlockSpec(memory_space=pl.ANY),
        out_shape=pltpu.HBM(x.shape, BF),
        scratch_shapes=[
            pltpu.VMEM(s.shape, BF),
            pltpu.VMEM(x.shape, BF),
            pltpu.SemaphoreType.DMA((s.shape[0],)),
            pltpu.SemaphoreType.DMA((s.shape[0] // 2,)),
        ],
        compiler_params=LIMIT,
        name="legendre",
    )(mine, *on_chip(x, a), *off_chip(s), *on_chip(filters))


def synth_kernel(table_ref, x_ref, field_ref, *rest, place):
    out_ref, part_ref, rows, cols = rest[-4:]
    count, chan, _ = part_ref.shape
    bands = x_ref.shape[0]
    pieces = table_ref.shape[0] // bands
    tiles = rows.shape[0]
    for q in range(tiles):
        tile = x_ref[:, place, :, q * LANES : (q + 1) * LANES]
        rows[q] = tile.reshape(count * bands, LANES).astype(F32)
    for t in range(count):
        line = [rows[q, pl.ds(t, bands, count), :] for q in range(tiles)]
        line = jnp.concatenate(line, 1).astype(BF)
        for j in range(pieces):
            piece = line[:, j * chan : (j + 1) * chan]
            cols[j * bands : (j + 1) * bands, t * chan : (t + 1) * chan] = piece
    total = lax.dot_general(
        cols[...], table_ref[...], (((0,), (0,)), ((), ())), preferred_element_type=F32
    )
    for t in range(count):
        at = place * count + t
        done = (field_ref[at].astype(F32) + total[t * chan : (t + 1) * chan]).astype(BF)
        out_ref[at] = done
        part_ref[t] = done


def synthesise(table, x, field, place, filled=None):
    _, chan, lon = field.shape
    bands, _, count, width = x.shape
    tiles = width // LANES
    more = [] if filled is None else [filled]
    return pl.pallas_call(
        functools.partial(synth_kernel, place=place),
        in_specs=[VMEM] * (3 + len(more)),
        out_specs=[VMEM, VMEM],
        out_shape=[pltpu.VMEM(field.shape, BF), pltpu.VMEM((count, chan, lon), BF)],
        input_output_aliases={3: 0} if more else {},
        scratch_shapes=[
            pltpu.VMEM((tiles, count * bands, LANES), F32),
            pltpu.VMEM((table.shape[0], count * chan), BF),
        ],
        compiler_params=LIMIT,
        name="synthesise",
    )(*on_chip(table, x, field, *more))


def crps_kernel(own_ref, near_ref, far_ref, far_near_ref, seen_ref, *rest, start):
    out_ref = rest[-1]
    t = pl.program_id(0)
    own = own_ref[start + t].astype(F32)

    def slope(other):
        d = own - other.astype(F32)
        return d * lax.rsqrt(d * d + smooth_sq)

    pair = slope(near_ref[start + t]) + slope(far_ref[t]) + slope(far_near_ref[t])
    out_ref[0] = (slope(seen_ref[start + t]) - pair * (1.0 / ENS)).astype(BF)


def crps(own, near, far, far_near, seen, start, filled=None):
    lat, chan, lon = far.shape
    more = [] if filled is None else [filled]
    return pl.pallas_call(
        functools.partial(crps_kernel, start=start),
        grid=(lat,),
        in_specs=[VMEM] * 5 + [pl.BlockSpec(memory_space=pl.ANY)] * len(more),
        out_specs=pl.BlockSpec((1, chan, lon), lambda t: (t + start, 0, 0)),
        out_shape=jax.ShapeDtypeStruct(own.shape, BF),
        input_output_aliases={5: 0} if more else {},
        compiler_params=LIMIT,
        name="crps",
    )(*on_chip(own, near, far, far_near, seen), *more)


def body(field, target, slot_orders, analysis, synthesis, degree_filter):
    lat, chan, _ = field.shape[1:]
    mine_count, degrees = analysis.shape[0], analysis.shape[2]
    bands = lax.axis_size("polar")
    ens = lax.axis_size("ens")
    width = 2 * mine_count * chan
    packed = (bands, lat // 2, 2, width)
    flat = (bands * lat // 2, 2, width)
    spectral = analyse(slot_orders, field[0], bands, degrees).reshape(packed)
    got = lax.all_to_all(spectral, "polar", split_axis=0, concat_axis=0, tiled=True)
    group = (lax.axis_index("ens") // ENS).reshape(1)
    mine = lax.dynamic_slice_in_dim(slot_orders, lax.axis_index("polar") * mine_count, mine_count)
    ready = tables(group, jnp.swapaxes(analysis, 1, 2), synthesis, degree_filter.T, chan)
    got, mine, *ready = lax.optimization_barrier((got, mine, *ready))
    out = legendre(mine, got.reshape(flat), *ready)
    back = lax.all_to_all(out.reshape(packed), "polar", split_axis=0, concat_axis=0, tiled=True)
    ready = scene(group, slot_orders, jnp.swapaxes(target, 1, 2), field[0], bands, degrees)
    back, inverse, seen, near_field = lax.optimization_barrier((back, *ready))
    across = [(i, i ^ 2) for i in range(ens)]
    beside = [(i, i ^ 1) for i in range(ens)]
    count = 2
    prediction = gradient = None
    fars = []
    for k in range(CHUNKS):
        prediction, part = synthesise(
            inverse, back, near_field, k, prediction
        )
        fars.append(lax.ppermute(part, "ens", across))
    near = lax.ppermute(prediction, "ens", beside)
    for k, far in enumerate(fars):
        far_near = lax.ppermute(far, "ens", beside)
        gradient = crps(prediction, near, far, far_near, seen, k * count, gradient)
    return prediction[None], gradient[None]


def solution(mesh):
    in_specs = (
        P("ens", "polar", None, None),
        P("polar", None, None),
        P(),
        P("polar", None, None),
        P("polar", None, None),
        P(),
    )
    out_specs = (P("ens", "polar", None, None), P("ens", "polar", None, None))
    return jax.shard_map(body, mesh=mesh, in_specs=in_specs, out_specs=out_specs, check_vma=False)
```

time: 189 us -> 176 us (0.931)
  local copies, waits for them, and re-layouts: 8.29 us -> 1.68 us
  Pallas kernels: 30.3 us -> 23.7 us
  waiting for transfers between devices: 85.6 us -> 88.8 us
  matrix products: 2.1 us -> 0 us
    pallas_call x8 -> x9, Pallas kernels: 25.5 us -> 20.1 us  [the longest x1 4.86 us: legendre(): pl.pallas_call(legendre_kernel, in_specs=[pl.BlockSpec(memory_space=pltpu...]
    unnamed x7, local copies, waits for them, and re-layouts: 5.23 us -> 1.6 us
    all_to_all x1, waiting for transfers between devices: 38.1 us -> 40.8 us  [body(): lax.all_to_all(spectral, 'polar', split_axis=0, concat_axis=0, tiled=True)]
    dot_general x1 -> x0, matrix products: 2.1 us -> none  [body(): jnp.einsum('qc,tck->tqk', pick, target, preferred_element_type=F32)]
  transfers between devices with their start and end apart: 9 -> 9, of which waited for: 5 -> 5; matrix products, arithmetic and copies ran while one was open for 5% -> 1% of each run, Pallas kernels for 4% -> 7%
where the time goes in v4:
time: 176 us; the launch traced here: 175 us
  waiting for transfers between devices  88.8 us (50%)
  starting transfers between devices  60.4 us (34%)
  Pallas kernels  23.7 us (13%)
    all_to_all x1, waiting for transfers between devices, body(): lax.all_to_all(spectral, 'polar', split_axis=0, concat_axis=0, tiled=True)  40.8 us
    all_to_all x1, waiting for transfers between devices, body(): lax.all_to_all(out.reshape(packed), 'polar', split_axis=0, concat_axis=0,...  39.9 us
    all_to_all x1, starting transfers between devices, body(): lax.all_to_all(spectral, 'polar', split_axis=0, concat_axis=0, tiled=True)  25.6 us
    all_to_all x1, starting transfers between devices, body(): lax.all_to_all(out.reshape(packed), 'polar', split_axis=0, concat_axis=0,...  10.6 us
    ppermute x3, starting transfers between devices, body(): far_near = lax.ppermute(far, 'ens', beside)  9.25 us
    ppermute x3, starting transfers between devices, body(): fars.append(lax.ppermute(part, 'ens', across))  8.4 us
    ppermute x3, waiting for transfers between devices, body(): fars.append(lax.ppermute(part, 'ens', across))  8.16 us
    ppermute x1, starting transfers between devices, body(): near = lax.ppermute(prediction, 'ens', beside)  6.58 us
  transfers between devices with their start and end apart: 9, of which 5 were waited for; matrix products, arithmetic and copies ran while one was open for 1% of the time, Pallas kernels for 7%

profile of v4, /device:TPU:1, one launch (start us, length us, event | category | flops | bytes accessed | tf_op | source)
XLA Modules:
  0.0 175.4 jit_solution(1960395077368275034)
XLA Ops:
  0.6 0.7 copy-done.1
  1.3 3.6 %analyse.1 = bf16[192,2,1152]{2,1,0:T(2,128)(2,1)} custom-call(s32[384]{0:T(512)S(1)} %copy-done.1, bf16[6,96,720]{2,1,0:T(8,128)(2,1)} %bitcast.15), custom_call_target="tpu_custom_call" | custom-call | tf_op jit(solution)/shard_map/analyse/pallas_call | solution.py:121
  4.9 25.6 %all-to-all-start = ((bf16[64,3,2,1152]{3,2,1,0:T(2,128)(2,1)}), bf16[64,3,2,1152]{3,2,1,0:T(2,128)(2,1)S(1)}, u32[]{:S(2)}, u32[]{:S(2)}) async-start(bf16[64,3,2,1152]{3,2,1,0:T(2,128)(2,1)} %bitcast.13), calls=%async_computation | async-start | bytes 1769472 | tf_op jit(solution)/shard_map/all_to_all | solution.py:349
  30.5 0.1 dynamic_slice.3.mine_ref
  30.6 4.3 %tables.1 = (bf16[6,360,384]{2,1,0:T(8,128)(2,1)S(1)}, bf16[6,384,360]{2,1,0:T(8,128)(2,1)}, f32[360,96]{1,0:T(8,128)S(1)}) custom-call(s32[1]{0:T(128)} %bitcast.2.group_ref, bf16[6,360,384]{2,1,0:T(8,128)(2,1)} %bitcast.18, bf16[6,360,384]{2,1,0:T(8,128)(2,1)} %s_ref.1, f32[360,384]{1,0:T(8,128)} %bitcast.19), custom_call_target="tpu_custom_call" | custom-call | tf_op jit(solution)/shard_map/tables/pallas_call | solution.py:155
  34.9 40.8 %all-to-all-done = bf16[64,3,2,1152]{3,2,1,0:T(2,128)(2,1)S(1)} async-done(((bf16[64,3,2,1152]{3,2,1,0:T(2,128)(2,1)}), bf16[64,3,2,1152]{3,2,1,0:T(2,128)(2,1)S(1)}, u32[]{:S(2)}, u32[]{:S(2)}) %all-to-all-start) | async-done | bytes 884768 | tf_op jit(solution)/shard_map/all_to_all | solution.py:349
  75.7 4.9 %legendre.1 = bf16[192,2,1152]{2,1,0:T(2,128)(2,1)} custom-call(s32[6]{0:T(128)S(1)} %dynamic_slice.3.mine_ref, bf16[192,2,1152]{2,1,0:T(2,128)(2,1)S(1)} %bitcast.11, bf16[6,360,384]{2,1,0:T(8,128)(2,1)S(1)} %get-tuple-element.28.a_ref, bf16[6,384,360]{2,1,0:T(8,128)(2,1)} %get-tuple-element.29.source_ref, f32[360,96]{1,0:T(8,128)S(1)} %get-tuple-element.30.filter_ref), custom_call_target="tpu_custom_call" | custom-call | tf_op jit(solution)/shard_map/legendre/pallas_call | solution.py:245
  80.5 10.6 %all-to-all-start.1 = ((bf16[64,3,2,1152]{3,2,1,0:T(2,128)(2,1)}), bf16[64,3,2,1152]{3,2,1,0:T(2,128)(2,1)S(1)}, u32[]{:S(2)}, u32[]{:S(2)}) async-start(bf16[64,3,2,1152]{3,2,1,0:T(2,128)(2,1)} %bitcast.14), calls=%async_computation.1 | async-start | bytes 1769472 | tf_op jit(solution)/shard_map/all_to_all | solution.py:355
  91.1 4.8 %scene.1 = (bf16[768,720]{1,0:T(8,128)(2,1)S(1)}, bf16[6,96,720]{2,1,0:T(8,128)(2,1)}, bf16[6,96,720]{2,1,0:T(8,128)(2,1)S(1)}) custom-call(s32[1]{0:T(128)} %bitcast.2.group_ref, s32[384]{0:T(512)S(1)} %copy-done.2, bf16[6,720,384]{2,1,0:T(8,128)(2,1)} %bitcast.17, bf16[6,96,720]{2,1,0:T(8,128)(2,1)} %bitcast.16), custom_call_target="tpu_custom_call" | custom-call | tf_op jit(solution)/shard_map/scene/pallas_call | solution.py:195
  95.9 39.9 %all-to-all-done.1.x_ref = bf16[64,3,2,1152]{3,2,1,0:T(2,128)(2,1)S(1)} async-done(((bf16[64,3,2,1152]{3,2,1,0:T(2,128)(2,1)}), bf16[64,3,2,1152]{3,2,1,0:T(2,128)(2,1)S(1)}, u32[]{:S(2)}, u32[]{:S(2)}) %all-to-all-start.1) | async-done | bytes 884768 | tf_op jit(solution)/shard_map/all_to_all | solution.py:355
  135.8 0.8 synthesise.3
  136.6 0.8 synthesise.4
  137.4 0.8 synthesise.5
  138.2 0.0 copy-start
  138.2 6.6 %collective-permute-start = (bf16[6,96,720]{2,1,0:T(8,128)(2,1)S(1)}, bf16[6,96,720]{2,1,0:T(8,128)(2,1)S(1)}, u32[]{:S(2)}, u32[]{:S(2)}) collective-permute-start(bf16[6,96,720]{2,1,0:T(8,128)(2,1)S(1)} %get-tuple-element.39.own_ref), channel_id=1, source_target_pairs={{0,64},{64,0},{128,192},{192,128},{256,320},{320,256},{384,448},{4... | collective-permute-start | bytes 2488328 | tf_op jit(solution)/shard_map/ppermute | solution.py:368
  144.8 3.1 %collective-permute-start.5 = (bf16[2,96,720]{2,1,0:T(8,128)(2,1)S(1)}, bf16[2,96,720]{2,1,0:T(8,128)(2,1)S(1)}, u32[]{:S(2)}, u32[]{:S(2)}) collective-permute-start(bf16[2,96,720]{2,1,0:T(8,128)(2,1)S(1)} %get-tuple-element.43), channel_id=1, source_target_pairs={{0,128},{64,192},{128,0},{192,64},{256,384},{320,448},{384,256},{4... | collective-permute-start | bytes 829448 | tf_op jit(solution)/shard_map/ppermute | solution.py:367
  147.9 2.2 %collective-permute-start.3 = (bf16[2,96,720]{2,1,0:T(8,128)(2,1)S(1)}, bf16[2,96,720]{2,1,0:T(8,128)(2,1)S(1)}, u32[]{:S(2)}, u32[]{:S(2)}) collective-permute-start(bf16[2,96,720]{2,1,0:T(8,128)(2,1)S(1)} %get-tuple-element.42), channel_id=1, source_target_pairs={{0,128},{64,192},{128,0},{192,64},{256,384},{320,448},{384,256},{4... | collective-permute-start | bytes 829448 | tf_op jit(solution)/shard_map/ppermute | solution.py:367
  150.1 3.1 %collective-permute-start.1 = (bf16[2,96,720]{2,1,0:T(8,128)(2,1)S(1)}, bf16[2,96,720]{2,1,0:T(8,128)(2,1)S(1)}, u32[]{:S(2)}, u32[]{:S(2)}) collective-permute-start(bf16[2,96,720]{2,1,0:T(8,128)(2,1)S(1)} %get-tuple-element.40), channel_id=1, source_target_pairs={{0,128},{64,192},{128,0},{192,64},{256,384},{320,448},{384,256},{4... | collective-permute-start | bytes 829448 | tf_op jit(solution)/shard_map/ppermute | solution.py:367
  153.2 2.0 %collective-permute-done.5.far_ref = bf16[2,96,720]{2,1,0:T(8,128)(2,1)S(1)} collective-permute-done((bf16[2,96,720]{2,1,0:T(8,128)(2,1)S(1)}, bf16[2,96,720]{2,1,0:T(8,128)(2,1)S(1)}, u32[]{:S(2)}, u32[]{:S(2)}) %collective-permute-start.5) | collective-permute-done | bytes 276512 | tf_op jit(solution)/shard_map/ppermute | solution.py:367
  155.2 3.2 %collective-permute-start.6 = (bf16[2,96,720]{2,1,0:T(8,128)(2,1)S(1)}, bf16[2,96,720]{2,1,0:T(8,128)(2,1)S(1)}, u32[]{:S(2)}, u32[]{:S(2)}) collective-permute-start(bf16[2,96,720]{2,1,0:T(8,128)(2,1)S(1)} %collective-permute-done.5.far_ref), channel_id=1, source_target_pairs={{0,64},{64,0},{128,192},{192,128},{256,320},{320,256},{384,448},{4... | collective-permute-start | bytes 829448 | tf_op jit(solution)/shard_map/ppermute | solution.py:370
  158.5 3.1 %collective-permute-done.3.far_ref = bf16[2,96,720]{2,1,0:T(8,128)(2,1)S(1)} collective-permute-done((bf16[2,96,720]{2,1,0:T(8,128)(2,1)S(1)}, bf16[2,96,720]{2,1,0:T(8,128)(2,1)S(1)}, u32[]{:S(2)}, u32[]{:S(2)}) %collective-permute-start.3) | collective-permute-done | bytes 276512 | tf_op jit(solution)/shard_map/ppermute | solution.py:367
  161.6 3.2 %collective-permute-start.4 = (bf16[2,96,720]{2,1,0:T(8,128)(2,1)S(1)}, bf16[2,96,720]{2,1,0:T(8,128)(2,1)S(1)}, u32[]{:S(2)}, u32[]{:S(2)}) collective-permute-start(bf16[2,96,720]{2,1,0:T(8,128)(2,1)S(1)} %collective-permute-done.3.far_ref), channel_id=1, source_target_pairs={{0,64},{64,0},{128,192},{192,128},{256,320},{320,256},{384,448},{4... | collective-permute-start | bytes 829448 | tf_op jit(solution)/shard_map/ppermute | solution.py:370
  164.8 3.1 %collective-permute-done.1.far_ref = bf16[2,96,720]{2,1,0:T(8,128)(2,1)S(1)} collective-permute-done((bf16[2,96,720]{2,1,0:T(8,128)(2,1)S(1)}, bf16[2,96,720]{2,1,0:T(8,128)(2,1)S(1)}, u32[]{:S(2)}, u32[]{:S(2)}) %collective-permute-start.1) | collective-permute-done | bytes 276512 | tf_op jit(solution)/shard_map/ppermute | solution.py:367
  167.9 2.8 %collective-permute-start.2 = (bf16[2,96,720]{2,1,0:T(8,128)(2,1)S(1)}, bf16[2,96,720]{2,1,0:T(8,128)(2,1)S(1)}, u32[]{:S(2)}, u32[]{:S(2)}) collective-permute-start(bf16[2,96,720]{2,1,0:T(8,128)(2,1)S(1)} %collective-permute-done.1.far_ref), channel_id=1, source_target_pairs={{0,64},{64,0},{128,192},{192,128},{256,320},{320,256},{384,448},{4... | collective-permute-start | bytes 829448 | tf_op jit(solution)/shard_map/ppermute | solution.py:370
  170.7 0.9 copy.16
  171.6 0.0 collective-permute-done.6.far_near_ref
  171.6 0.0 collective-permute-done.near_ref
  171.6 1.3 crps.3.rest_0_
  172.9 0.0 collective-permute-done.4.far_near_ref
  172.9 1.2 crps.4.rest_0_
  174.1 0.0 collective-permute-done.2.far_near_ref
  174.1 1.2 crps.5
  (4 shorter events, 0.0 us)
Async XLA Ops:
  0.6 0.7 copy-start.1
  1.3 29.2 %copy-start.2 = (s32[384]{0:T(512)S(1)}, s32[384]{0:T(512)}, u32[]{:S(2)}) copy-start(s32[384]{0:T(512)} %orders_ref.3) | copy-start | bytes 4612
  4.9 70.7 %all-to-all-start = ((bf16[64,3,2,1152]{3,2,1,0:T(2,128)(2,1)}), bf16[64,3,2,1152]{3,2,1,0:T(2,128)(2,1)S(1)}, u32[]{:S(2)}, u32[]{:S(2)}) async-start(bf16[64,3,2,1152]{3,2,1,0:T(2,128)(2,1)} %bitcast.13), calls=%async_computation | async-start | bytes 1769472 | tf_op jit(solution)/shard_map/all_to_all | solution.py:349
  80.5 55.3 %all-to-all-start.1 = ((bf16[64,3,2,1152]{3,2,1,0:T(2,128)(2,1)}), bf16[64,3,2,1152]{3,2,1,0:T(2,128)(2,1)S(1)}, u32[]{:S(2)}, u32[]{:S(2)}) async-start(bf16[64,3,2,1152]{3,2,1,0:T(2,128)(2,1)} %bitcast.14), calls=%async_computation.1 | async-start | bytes 1769472 | tf_op jit(solution)/shard_map/all_to_all | solution.py:355
  138.2 33.4 %copy-start = (bf16[6,96,720]{2,1,0:T(8,128)(2,1)S(1)}, bf16[6,96,720]{2,1,0:T(8,128)(2,1)}, u32[]{:S(2)}) copy-start(bf16[6,96,720]{2,1,0:T(8,128)(2,1)} %get-tuple-element.41.seen_ref) | copy-start | bytes 2488324
  138.2 33.4 %collective-permute-start = (bf16[6,96,720]{2,1,0:T(8,128)(2,1)S(1)}, bf16[6,96,720]{2,1,0:T(8,128)(2,1)S(1)}, u32[]{:S(2)}, u32[]{:S(2)}) collective-permute-start(bf16[6,96,720]{2,1,0:T(8,128)(2,1)S(1)} %get-tuple-element.39.own_ref), channel_id=1, source_target_pairs={{0,64},{64,0},{128,192},{192,128},{256,320},{320,256},{384,448},{4... | collective-permute-start | bytes 2488328 | tf_op jit(solution)/shard_map/ppermute | solution.py:368
  144.8 10.4 %collective-permute-start.5 = (bf16[2,96,720]{2,1,0:T(8,128)(2,1)S(1)}, bf16[2,96,720]{2,1,0:T(8,128)(2,1)S(1)}, u32[]{:S(2)}, u32[]{:S(2)}) collective-permute-start(bf16[2,96,720]{2,1,0:T(8,128)(2,1)S(1)} %get-tuple-element.43), channel_id=1, source_target_pairs={{0,128},{64,192},{128,0},{192,64},{256,384},{320,448},{384,256},{4... | collective-permute-start | bytes 829448 | tf_op jit(solution)/shard_map/ppermute | solution.py:367
  147.9 13.6 %collective-permute-start.3 = (bf16[2,96,720]{2,1,0:T(8,128)(2,1)S(1)}, bf16[2,96,720]{2,1,0:T(8,128)(2,1)S(1)}, u32[]{:S(2)}, u32[]{:S(2)}) collective-permute-start(bf16[2,96,720]{2,1,0:T(8,128)(2,1)S(1)} %get-tuple-element.42), channel_id=1, source_target_pairs={{0,128},{64,192},{128,0},{192,64},{256,384},{320,448},{384,256},{4... | collective-permute-start | bytes 829448 | tf_op jit(solution)/shard_map/ppermute | solution.py:367
  150.1 17.8 %collective-permute-start.1 = (bf16[2,96,720]{2,1,0:T(8,128)(2,1)S(1)}, bf16[2,96,720]{2,1,0:T(8,128)(2,1)S(1)}, u32[]{:S(2)}, u32[]{:S(2)}) collective-permute-start(bf16[2,96,720]{2,1,0:T(8,128)(2,1)S(1)} %get-tuple-element.40), channel_id=1, source_target_pairs={{0,128},{64,192},{128,0},{192,64},{256,384},{320,448},{384,256},{4... | collective-permute-start | bytes 829448 | tf_op jit(solution)/shard_map/ppermute | solution.py:367
  155.2 16.3 %collective-permute-start.6 = (bf16[2,96,720]{2,1,0:T(8,128)(2,1)S(1)}, bf16[2,96,720]{2,1,0:T(8,128)(2,1)S(1)}, u32[]{:S(2)}, u32[]{:S(2)}) collective-permute-start(bf16[2,96,720]{2,1,0:T(8,128)(2,1)S(1)} %collective-permute-done.5.far_ref), channel_id=1, source_target_pairs={{0,64},{64,0},{128,192},{192,128},{256,320},{320,256},{384,448},{4... | collective-permute-start | bytes 829448 | tf_op jit(solution)/shard_map/ppermute | solution.py:370
  161.6 11.3 %collective-permute-start.4 = (bf16[2,96,720]{2,1,0:T(8,128)(2,1)S(1)}, bf16[2,96,720]{2,1,0:T(8,128)(2,1)S(1)}, u32[]{:S(2)}, u32[]{:S(2)}) collective-permute-start(bf16[2,96,720]{2,1,0:T(8,128)(2,1)S(1)} %collective-permute-done.3.far_ref), channel_id=1, source_target_pairs={{0,64},{64,0},{128,192},{192,128},{256,320},{320,256},{384,448},{4... | collective-permute-start | bytes 829448 | tf_op jit(solution)/shard_map/ppermute | solution.py:370
  167.9 6.2 %collective-permute-start.2 = (bf16[2,96,720]{2,1,0:T(8,128)(2,1)S(1)}, bf16[2,96,720]{2,1,0:T(8,128)(2,1)S(1)}, u32[]{:S(2)}, u32[]{:S(2)}) collective-permute-start(bf16[2,96,720]{2,1,0:T(8,128)(2,1)S(1)} %collective-permute-done.1.far_ref), channel_id=1, source_target_pairs={{0,64},{64,0},{128,192},{192,128},{256,320},{320,256},{384,448},{4... | collective-permute-start | bytes 829448 | tf_op jit(solution)/shard_map/ppermute | solution.py:370
